TPU v7x, 512 devices: a whole 4x4x16 slice. The times are simulated.
512 devices in a mesh: tm: 128 (over x, z, core), head: 4 (over y).
Axes of the slice: x: 4, y: 4, z: 16, core: 2. Of those that a mesh axis runs over, the one named last changes fastest.
Arguments:
- latent: bfloat16 [65536, 1024], P('tm', 'head'), may hold values from -6 to 6
- timestep: int32 [1], replicated, may hold values from 0 to 999
- in_gain: float32 [1024], replicated, may hold values from 0.1 to 1.9
- w_x: bfloat16 [1024, 2048], P(None, 'head'), may hold values from -0.1875 to 0.1875
- w_z: bfloat16 [1024, 2048], P(None, 'head'), may hold values from -0.1875 to 0.1875
- w_bc: bfloat16 [1024, 256], replicated, may hold values from -0.1875 to 0.1875
- w_dt: bfloat16 [1024, 32], P(None, 'head'), may hold values from -0.1875 to 0.1875
- conv_x: float32 [4, 2048], P(None, 'head'), may hold values from -3 to 3
- conv_bc: float32 [4, 256], replicated, may hold values from -3 to 3
- dt_bias: float32 [32], P('head'), may hold values from -1 to 0.5
- a_log: float32 [32], P('head'), may hold values from -13 to -1, as said below
- d_skip: float32 [32], P('head'), may hold values from 4 to 64
- norm_gain: float32 [2048], P('head'), may hold values from 0.1 to 1.9
- w_out: bfloat16 [2048, 1024], P('head'), may hold values from -0.125 to 0.125
- w_mix: bfloat16 [1024, 1024], P(None, 'head'), may hold values from -0.1875 to 0.1875
Outputs:
- denoised: bfloat16 [65536, 1024], P('tm', 'head')
Inputs may be any that keep to these rules, and one draw needn't show every extreme that they name: `a_log`: the logarithm of each head's decay rate.
All inputs are finite; a program needn't handle non-finite values.
Results may differ from a plain program's by a relative error of at most 0.012.
Values may be sent and summed in bfloat16 or wider, within the bound.
A program may use at most 128 MiB of HBM per device.

v0:
```python
import math

import jax
import jax.numpy as jnp
from jax import lax
from jax.sharding import PartitionSpec as P

BLOCK = 256


def from_behind(block, axis, distance):
    devices = range(lax.axis_size(axis))
    route = [(i - distance, i) for i in devices if i - distance in devices]
    return lax.ppermute(block, axis, route)


def prefix(part, axis, combine, identity):
    place = lax.axis_index(axis)
    gathered = jax.tree.map(lambda a: lax.all_gather(a, axis), part)
    state = jax.tree.map(lambda a, e: jnp.zeros_like(a) + jnp.asarray(e, a.dtype), part, identity)

    def one(hop, state):
        return combine(
            state, jax.tree.map(lambda a: lax.dynamic_index_in_dim(a, hop, 0, False), gathered)
        )

    return lax.fori_loop(0, place, one, state)


def sinusoid(timestep, width):
    half = width // 2
    freq = jnp.exp(-math.log(10000.0) * jnp.arange(half, dtype=jnp.float32) / half)
    angle = timestep.astype(jnp.float32)[0] * freq
    return jnp.concatenate([jnp.sin(angle), jnp.cos(angle)])


def causal_conv(rows, rim, kernel):
    padded = jnp.concatenate([rim, rows], axis=0)
    count = rows.shape[0]
    total = jnp.zeros(rows.shape, jnp.float32)
    for k in range(kernel.shape[0]):
        total = total + padded[k : k + count].astype(jnp.float32) * kernel[k]
    return jax.nn.silu(total).astype(jnp.bfloat16)


def block_terms(xa, bmat, cmat, dt, la):
    steps = xa.shape[0]
    cum = jnp.cumsum(la, axis=0)
    scores = jnp.dot(cmat, bmat.T, preferred_element_type=jnp.float32)
    rowid = lax.broadcasted_iota(jnp.int32, (steps, steps), 0)
    colid = lax.broadcasted_iota(jnp.int32, (steps, steps), 1)
    causal = rowid >= colid
    cumt = cum.T
    seg = cumt[:, :, None] - cumt[:, None, :]
    decay = jnp.exp(jnp.where(causal[None], seg, -jnp.inf))
    mixw = (scores[None] * decay * dt.T[:, None, :]).astype(jnp.bfloat16)
    ydiag = jnp.einsum("hij,jhp->ihp", mixw, xa, preferred_element_type=jnp.float32)
    tail = jnp.exp(cum[-1][None, :] - cum) * dt
    weighted = (bmat.astype(jnp.float32)[:, None, :] * tail[:, :, None]).astype(jnp.bfloat16)
    state = jnp.einsum("jhn,jhp->hnp", weighted, xa, preferred_element_type=jnp.float32)
    total = jnp.exp(cum[-1])
    return (ydiag, state, total, cum)


def block_output(ydiag, cum, cmat, hin, xa, d_skip):
    yoff = jnp.einsum(
        "in,hnp->ihp", cmat, hin.astype(jnp.bfloat16), preferred_element_type=jnp.float32
    )
    yoff = yoff * jnp.exp(cum)[:, :, None]
    return ydiag + yoff + d_skip[None, :, None] * xa.astype(jnp.float32)


def combine_states(earlier, later):
    return (earlier[0] * later[0], earlier[1] * later[0][:, None, None] + later[1])


def shards(
    latent,
    timestep,
    in_gain,
    w_x,
    w_z,
    w_bc,
    w_dt,
    conv_x,
    conv_bc,
    dt_bias,
    a_log,
    d_skip,
    norm_gain,
    w_out,
    w_mix,
):
    whole = lax.all_gather(latent, "head", axis=1, tiled=True)
    u = whole.astype(jnp.float32) + sinusoid(timestep, whole.shape[1])[None, :]
    normed = (u * lax.rsqrt(jnp.mean(u * u, axis=1, keepdims=True) + 1e-05) * in_gain).astype(
        jnp.bfloat16
    )
    xs = jnp.dot(normed, w_x, preferred_element_type=jnp.float32).astype(jnp.bfloat16)
    gate = jnp.dot(normed, w_z, preferred_element_type=jnp.float32).astype(jnp.bfloat16)
    bc = jnp.dot(normed, w_bc, preferred_element_type=jnp.float32).astype(jnp.bfloat16)
    dt_raw = jnp.dot(normed, w_dt, preferred_element_type=jnp.float32)
    width = conv_x.shape[0] - 1
    steps_dev = xs.shape[0]
    rim_x, rim_bc = from_behind((xs[steps_dev - width :], bc[steps_dev - width :]), "tm", 1)
    xa = causal_conv(xs, rim_x, conv_x)
    bca = causal_conv(bc, rim_bc, conv_bc)
    state_n = w_bc.shape[1] // 2
    bmat = bca[:, :state_n]
    cmat = bca[:, state_n:]
    dt = jax.nn.softplus(dt_raw + dt_bias)
    la = dt * -jnp.exp(a_log)
    heads = dt.shape[1]
    hdim = xa.shape[1] // heads
    blocks = steps_dev // BLOCK
    xa4 = xa.reshape(blocks, BLOCK, heads, hdim)
    b3 = bmat.reshape(blocks, BLOCK, state_n)
    c3 = cmat.reshape(blocks, BLOCK, state_n)
    dt3 = dt.reshape(blocks, BLOCK, heads)
    la3 = la.reshape(blocks, BLOCK, heads)
    ydiag, states, totals, cums = jax.vmap(block_terms)(xa4, b3, c3, dt3, la3)
    run_decay = jnp.ones((heads,), jnp.float32)
    run_state = jnp.zeros((heads, state_n, hdim), jnp.float32)
    before = []
    for index in range(blocks):
        before.append((run_decay, run_state))
        run_decay, run_state = combine_states(
            (run_decay, run_state), (totals[index], states[index])
        )
    identity = (jnp.ones_like(run_decay), jnp.zeros_like(run_state))
    _, incoming = prefix((run_decay, run_state), "tm", combine_states, identity)
    hins = jnp.stack([incoming * pair[0][:, None, None] + pair[1] for pair in before])
    ys = jax.vmap(block_output, in_axes=(0, 0, 0, 0, 0, None))(ydiag, cums, c3, hins, xa4, d_skip)
    y = ys.reshape(steps_dev, heads * hdim)
    gated = y * jax.nn.silu(gate.astype(jnp.float32))
    square = lax.psum(jnp.sum(gated * gated, axis=1), "head")
    inner = gated.shape[1] * lax.axis_size("head")
    yn = (gated * lax.rsqrt(square[:, None] / inner + 1e-05) * norm_gain).astype(jnp.bfloat16)
    mix_width = w_mix.shape[1]
    col_start = lax.axis_index("head") * mix_width
    share = steps_dev // lax.axis_size("head")
    row_start = lax.axis_index("head") * share
    summed = lax.psum_scatter(
        jnp.dot(yn, w_out, preferred_element_type=jnp.float32),
        "head",
        scatter_dimension=0,
        tiled=True,
    )
    hidden_rows = (lax.dynamic_slice_in_dim(u, row_start, share, 0) + summed).astype(jnp.bfloat16)
    piece = lax.all_gather(hidden_rows, "head", axis=0, tiled=True)
    own = lax.dynamic_slice_in_dim(piece, col_start, mix_width, 1).astype(jnp.float32)
    return (own + jnp.dot(piece, w_mix, preferred_element_type=jnp.float32)).astype(jnp.bfloat16)


def solution(mesh):
    in_specs = (
        P("tm", "head"),
        P(),
        P(),
        P(None, "head"),
        P(None, "head"),
        P(),
        P(None, "head"),
        P(None, "head"),
        P(),
        P("head"),
        P("head"),
        P("head"),
        P("head"),
        P("head", None),
        P(None, "head"),
    )
    out_specs = P("tm", "head")
    return jax.shard_map(shards, mesh=mesh, in_specs=in_specs, out_specs=out_specs, check_vma=False)
```

profile of v0, /device:TPU:1, one launch (start us, length us, event | category | flops | bytes accessed | tf_op | source)
XLA Modules:
  0.0 527.0 jit_solution(13383259743243343161)
XLA Ops:
  6.6 0.7 all-gather.5.cloned.1.call-update
  8.7 0.8 fusion.34
  9.5 0.9 fusion.33
  10.4 35.9 %all-gather.5.cloned.1.call-done = bf16[512,1024]{1,0:T(8,128)(2,1)} async-done(((bf16[512,256]{1,0:T(8,128)(2,1)}), bf16[512,1024]{1,0:T(8,128)(2,1)}) %all-gather.5.cloned.1.call-update) | async-done | bytes 1048592 | tf_op jit(solution)/shard_map/all_gather | solution.py:94
  46.3 2.9 convert_add_fusion
  49.7 1.2 reduce-window.6
  51.0 0.7 fusion.31
  52.0 1.6 convolution_convert_fusion.2
  53.5 5.3 %collective-permute-start.1 = (bf16[3,256]{1,0:T(4,128)(2,1)S(1)}, bf16[3,256]{1,0:T(4,128)(2,1)S(1)}, u32[]{:S(2)}, u32[]{:S(2)}) collective-permute-start(bf16[3,256]{1,0:T(4,128)(2,1)S(1)} %slice.106), channel_id=1, source_target_pairs={{0,4},{4,8},{8,12},{12,16},{16,20},{20,24},{24,28},{28,32},{32,36}... | collective-permute-start | bytes 4616 | tf_op jit(solution)/shard_map/ppermute | solution.py:14
  58.9 0.8 convolution_convert_fusion.1
  59.7 1.9 collective-permute-start
  62.0 0.7 fusion.32
  62.7 0.7 convert_element_type.96
  63.4 0.7 multiply_convert_fusion.12
  65.2 1.9 fusion.15
  67.2 0.8 slice_add_fusion
  68.7 78.9 %all-gather = f32[128,1,8]{2,1,0:T(1,128)S(1)} all-gather(f32[1,1,8]{2,1,0:T(1,128)S(1)} %get-tuple-element.98), channel_id=1, replica_groups=mesh['tm'=128,'head'=4] {'tm'}, dimensions={0}, use_global_device_ids=true | all-gather | bytes 4128 | tf_op jit(solution)/shard_map/all_gather | solution.py:19
  147.7 0.7 add_bitcast_fusion.1
  148.3 1.1 fusion.35
  149.4 115.6 %all-gather.7.cloned.1.call-done = f32[128,8,128,64]{2,3,1,0:T(8,128)} async-done(((f32[1,8,128,64]{2,3,1,0:T(8,128)}), f32[128,8,128,64]{2,3,1,0:T(8,128)}) %all-gather.7.cloned.1.call-update) | async-done | bytes 33554448 | tf_op jit(solution)/shard_map/all_gather | solution.py:19
  265.1 1.4 while.12
  265.1 1.0 constant_dynamic-slice_fusion.2
  267.7 3.0 fusion.9
  270.7 2.0 copy.60
  272.7 1.5 reshape.92
  274.2 2.9 multiply_reduce_fusion.1
  277.1 8.5 %psum.7 = f32[512]{0:T(512)S(1)} all-reduce(f32[512]{0:T(512)S(1)} %get-tuple-element.101), channel_id=1, replica_groups=mesh['tm'=128,'head'=4] {'head'}, use_global_device_ids=true, to_apply=%region_6.7 | all-reduce | flops 512 | bytes 4096 | tf_op jit(solution)/shard_map/psum | solution.py:136
  285.6 2.1 fusion.20
  287.8 198.5 %reduce-scatter.2.cloned.1.call-done = f32[128,1024]{1,0:T(8,128)} async-done(((f32[512,1024]{1,0:T(8,128)}), f32[128,1024]{1,0:T(8,128)}) %reduce-scatter.2.cloned.1.call-update) | async-done | bytes 524304 | tf_op jit(solution)/shard_map/reduce_scatter | solution.py:143
  486.3 2.0 add_convert_fusion
  488.3 29.7 %all-gather.9.cloned.1.call-done = bf16[512,1024]{1,0:T(8,128)(2,1)} async-done(((bf16[128,1024]{1,0:T(8,128)(2,1)}), bf16[512,1024]{1,0:T(8,128)(2,1)}) %all-gather.9.cloned.1.call-update) | async-done | bytes 1048592 | tf_op jit(solution)/shard_map/all_gather | solution.py:150
  518.0 2.4 fusion.10
  (71 shorter events, 5.6 us)
Async XLA Ops:
  6.5 279.0 %copy-start = (bf16[512,1024]{1,0:T(8,128)(2,1)S(1)}, bf16[512,1024]{1,0:T(8,128)(2,1)}, u32[]{:S(2)}) copy-start(bf16[512,1024]{1,0:T(8,128)(2,1)} %param.30) | copy-start | bytes 3145732
  6.5 42.6 %copy-start.14 = (f32[1024]{0:T(1024)S(1)}, f32[1024]{0:T(1024)}, u32[]{:S(2)}) copy-start(f32[1024]{0:T(1024)} %param.19) | copy-start | bytes 12292
  6.5 42.6 %copy-start.13 = (bf16[1024,8]{0,1:T(8,128)(2,1)S(1)}, bf16[1024,8]{0,1:T(8,128)(2,1)}, u32[]{:S(2)}) copy-start(bf16[1024,8]{0,1:T(8,128)(2,1)} %param.23) | copy-start | bytes 49156
  6.5 42.6 %copy-start.16 = (f32[8]{0:T(128)S(1)}, f32[8]{0:T(128)}, u32[]{:S(2)}) copy-start(f32[8]{0:T(128)} %param.26) | copy-start | bytes 100
  6.5 39.7 %all-gather.5.cloned.1.call-start = ((), (), s32[]{:S(2)}) async-start(), calls=%async_computation.1 | async-start | bytes 1310720 | tf_op jit(solution)/shard_map/all_gather | solution.py:94
  7.3 257.8 %all-gather.7.cloned.1.call-start = ((), (), s32[]{:S(2)}) async-start(), calls=%async_computation.2 | async-start | bytes 33816576 | tf_op jit(solution)/shard_map/all_gather | solution.py:19
  46.3 2.9 copy-start.3
  49.7 10.0 %copy-start.6 = (f32[512,8]{0,1:T(8,128)}, f32[512,8]{0,1:T(8,128)S(1)}, u32[]{:S(2)}) copy-start(f32[512,8]{0,1:T(8,128)S(1)} %get-tuple-element.100) | copy-start | bytes 49156
  49.7 9.2 %copy-start.11 = (bf16[1024,512]{1,0:T(8,128)(2,1)S(1)}, bf16[1024,512]{1,0:T(8,128)(2,1)}, u32[]{:S(2)}) copy-start(bf16[1024,512]{1,0:T(8,128)(2,1)} %param.20) | copy-start | bytes 3145732
  53.5 8.1 %collective-permute-start.1 = (bf16[3,256]{1,0:T(4,128)(2,1)S(1)}, bf16[3,256]{1,0:T(4,128)(2,1)S(1)}, u32[]{:S(2)}, u32[]{:S(2)}) collective-permute-start(bf16[3,256]{1,0:T(4,128)(2,1)S(1)} %slice.106), channel_id=1, source_target_pairs={{0,4},{4,8},{8,12},{12,16},{16,20},{20,24},{24,28},{28,32},{32,36}... | collective-permute-start | bytes 4616 | tf_op jit(solution)/shard_map/ppermute | solution.py:14
  59.7 3.7 collective-permute-start
  64.6 83.7 %copy-start.1 = (bf16[512,128]{1,0:T(8,128)(2,1)S(1)}, bf16[512,128]{1,0:T(8,128)(2,1)}, u32[]{:S(2)}) copy-start(bf16[512,128]{1,0:T(8,128)(2,1)} %get-tuple-element.87) | copy-start | bytes 393220
  68.0 418.3 %reduce-scatter.2.cloned.1.call-start = ((), (), s32[]{:S(2)}) async-start(), calls=%async_computation.3 | async-start | bytes 2621440 | tf_op jit(solution)/shard_map/reduce_scatter | solution.py:143
  266.5 0.9 copy-start.2
  266.5 1.2 copy-start.4
  266.7 1.0 copy-start.5
  266.7 1.0 copy-start.7
  266.7 1.0 copy-start.8
  266.7 1.0 copy-start.9
  272.7 1.5 copy-start.15
  274.2 11.4 %copy-start.10 = (f32[512]{0:T(512)S(1)}, f32[512]{0:T(512)}, u32[]{:S(2)}) copy-start(f32[512]{0:T(512)} %param.29) | copy-start | bytes 6148
  287.7 230.3 %copy-start.12 = (bf16[1024,256]{1,0:T(8,128)(2,1)S(1)}, bf16[1024,256]{1,0:T(8,128)(2,1)}, u32[]{:S(2)}) copy-start(bf16[1024,256]{1,0:T(8,128)(2,1)} %param.31) | copy-start | bytes 1572868
  287.7 230.3 %all-gather.9.cloned.1.call-start = ((), (), s32[]{:S(2)}) async-start(), calls=%async_computation.4 | async-start | bytes 1310720 | tf_op jit(solution)/shard_map/all_gather | solution.py:150
Sparse Core Ops, SparseCore 0:
  9.4 36.7 all-gather.4
  68.1 196.8 all-gather.6
  287.8 198.4 reduce-scatter.1
  488.4 29.5 all-gather.8
where the time goes:
time: 533 us; the launch traced here: 527 us
  waiting for transfers between devices  380 us (71%)
  blocking collectives  87.4 us (16%)
  matrix products  16.5 us (3%)
  between operations  14.1 us (3%)
  other arithmetic  11.7 us (2%)
  local copies, waits for them, and re-layouts  9.3 us (2%)
  starting transfers between devices  7.41 us (1%)
    reduce_scatter x1, waiting for transfers between devices, shards(): lax.psum_scatter(jnp.dot(yn, w_out, preferred_element_type=jnp.float32),...  199 us
    all_gather x1, waiting for transfers between devices, prefix(): gathered = jax.tree.map(lambda a: lax.all_gather(a, axis), part)  116 us
    all_gather x1, blocking collectives, prefix(): gathered = jax.tree.map(lambda a: lax.all_gather(a, axis), part)  78.9 us
    all_gather x1, waiting for transfers between devices, shards(): whole = lax.all_gather(latent, 'head', axis=1, tiled=True)  35.9 us
    all_gather x1, waiting for transfers between devices, shards(): piece = lax.all_gather(hidden_rows, 'head', axis=0, tiled=True)  29.7 us
  transfers between devices with their start and end apart: 6, of which 4 were waited for; matrix products, arithmetic and copies ran while one was open for 1% of the time, Pallas kernels for 0%

commit v1 on v0

v1 whole, which is shorter than its diff:
```python
import functools
import math

import jax
import jax.numpy as jnp
from jax import lax
from jax.experimental import pallas as pl
from jax.experimental.pallas import tpu as pltpu
from jax.sharding import PartitionSpec as P

BLOCK = 256
RIM = 16
LINE = 32
MESH = pl.DeviceIdType.MESH
VMEM = pl.BlockSpec(memory_space=pltpu.VMEM)
DMA = pltpu.SemaphoreType.DMA


def remote(src, dst, send, recv, **device):
    return pltpu.make_async_remote_copy(
        src_ref=src, dst_ref=dst, send_sem=send, recv_sem=recv, device_id=device, device_id_type=MESH
    )


def greet(devices, count):
    barrier = pltpu.get_barrier_semaphore()
    for device in devices:
        pl.semaphore_signal(barrier, inc=1, device_id=device, device_id_type=MESH)
    pl.semaphore_wait(barrier, count)


def aligned(index, size):
    return pl.ds(pl.multiple_of(index * size, size), size)


def gather_kernel(tms, heads, lat, out, own_sem, send, recv, rim_send, rim_recv):
    tm, me = lax.axis_index("tm"), lax.axis_index("head")
    right, left = lax.rem(me + 1, heads), lax.rem(me + heads - 1, heads)
    later, earlier = lax.rem(tm + 1, tms), lax.rem(tm + tms - 1, tms)
    rows, width = lat.shape
    half = rows // 2
    greet(
        [{"head": left}, {"head": right}] + [{"tm": earlier, "head": h} for h in range(heads)],
        2 + heads,
    )
    top, bottom = pl.ds(RIM, half), pl.ds(RIM + half, half)
    mine, lefts, rights = aligned(me, width), aligned(left, width), aligned(right, width)

    def own(rows_out, start, sem, to):
        return remote(
            lat.at[pl.ds(start, half)], out.at[rows_out, mine], send.at[sem], recv.at[sem], head=to
        )

    copies = [
        own(top, 0, 0, right),
        own(bottom, half, 1, left),
        own(bottom, half, 2, right),
        own(top, 0, 3, left),
    ]
    for copy in copies[:2]:
        copy.start()
    rims = [
        remote(
            lat.at[pl.ds(rows - RIM, RIM)],
            out.at[pl.ds(0, RIM), mine],
            rim_send.at[h],
            rim_recv.at[me],
            tm=later,
            head=h,
        )
        for h in range(heads)
    ]
    for copy in rims:
        copy.start()
    for copy in copies[2:]:
        copy.start()
    keep = pltpu.make_async_copy(lat, out.at[pl.ds(RIM, rows), mine], own_sem)
    keep.start()
    onward = [
        remote(out.at[top, lefts], out.at[top, lefts], send.at[4], recv.at[4], head=right),
        remote(out.at[bottom, rights], out.at[bottom, rights], send.at[5], recv.at[5], head=left),
    ]
    for copy, following in zip(copies[:2], onward):
        copy.wait_recv()
        following.start()
    for copy in copies[2:] + onward:
        copy.wait_recv()
    for h in range(heads):
        remote(
            lat.at[pl.ds(rows - RIM, RIM)],
            out.at[pl.ds(0, RIM), pl.ds(h * width, width)],
            rim_send.at[h],
            rim_recv.at[h],
            tm=later,
            head=h,
        ).wait_recv()
    for copy in copies + onward + rims:
        copy.wait_send()
    keep.wait()


def gather(lat, tms, heads):
    rows, width = lat.shape
    return pl.pallas_call(
        functools.partial(gather_kernel, tms, heads),
        out_shape=jax.ShapeDtypeStruct((rows + RIM, width * heads), lat.dtype),
        in_specs=[VMEM],
        out_specs=VMEM,
        scratch_shapes=[DMA, DMA((6,)), DMA((6,)), DMA((heads,)), DMA((heads,))],
        compiler_params=pltpu.CompilerParams(collective_id=0, has_side_effects=True),
        name="gather_rows",
    )(lat)


def scan_kernel(
    line, lines, piece, s, g, out, sin, gin, pre, dec, back, xt, xd, s_sem, g_sem, xt_sem, xd_sem, b_sem
):
    tm = lax.axis_index("tm")
    me, mine = lax.rem(tm, line), tm // line
    base = mine * line
    high, wide = piece
    stack = s.shape[0] // high

    def rows(k):
        return aligned(lax.rem(k, stack), high)

    def cols(k):
        return aligned(k // stack, wide)

    barrier = pltpu.get_barrier_semaphore()

    def other(o):
        return lax.rem(me + o, line)

    def other_line(o):
        return lax.rem(mine + o, lines)

    @pl.loop(1, line)
    def _(o):
        pl.semaphore_signal(barrier, inc=1, device_id={"tm": base + other(o)}, device_id_type=MESH)

    for o in range(1, lines):
        pl.semaphore_signal(
            barrier, inc=1, device_id={"tm": other_line(o) * line + me}, device_id_type=MESH
        )
    pl.semaphore_wait(barrier, line - 1 + lines - 1)

    def out_s(q):
        return remote(s.at[rows(q), cols(q)], sin.at[me], s_sem.at[0, q], s_sem.at[1, me], tm=base + q)

    def out_g(q):
        return remote(g.at[:, cols(q)], gin.at[me], g_sem.at[0, q], g_sem.at[1, me], tm=base + q)

    def in_s(q):
        return remote(s.at[rows(q), cols(q)], sin.at[q], s_sem.at[0, q], s_sem.at[1, q], tm=base + q)

    def in_g(q):
        return remote(g.at[:, cols(q)], gin.at[q], g_sem.at[0, q], g_sem.at[1, q], tm=base + q)

    @pl.loop(1, line)
    def _(o):
        q = other(o)
        out_g(q).start()
        out_s(q).start()

    sin[me] = s[rows(me), cols(me)]
    gin[me] = g[:, cols(me)]

    def step(k, carry):
        state, decay = carry

        @pl.when(k != me)
        def _():
            in_g(k).wait_recv()
            in_s(k).wait_recv()

        pre[k] = state
        dec[k] = decay
        factor = gin[k]
        return state * factor + sin[k].astype(jnp.float32), decay * factor

    state, decay = lax.fori_loop(
        0, line, step, (jnp.zeros((high, wide), jnp.float32), jnp.ones((1, wide), jnp.float32))
    )
    xt[mine] = state
    xd[mine] = decay

    def line_copies(q, slot):
        device = q * line + me
        return (
            remote(xt.at[slot], xt.at[slot], xt_sem.at[0, q], xt_sem.at[1, slot], tm=device),
            remote(xd.at[slot], xd.at[slot], xd_sem.at[0, q], xd_sem.at[1, slot], tm=device),
        )

    for o in range(1, lines):
        for copy in line_copies(other_line(o), mine):
            copy.start()
    for o in range(1, lines):
        for copy in line_copies(other_line(o), other_line(o)):
            copy.wait_recv()
    start = jnp.zeros((high, wide), jnp.float32)
    for k in range(lines):
        start = jnp.where(k < mine, start * xd[k] + xt[k], start)

    def final(k, carry):
        back[k] = (start * dec[k] + pre[k]).astype(back.dtype)
        return carry

    lax.fori_loop(0, line, final, 0)

    def out_b(q):
        return remote(
            back.at[q], out.at[rows(me), cols(me)], b_sem.at[0, q], b_sem.at[1, me], tm=base + q
        )

    def in_b(q):
        return remote(
            back.at[q], out.at[rows(q), cols(q)], b_sem.at[0, q], b_sem.at[1, q], tm=base + q
        )

    @pl.loop(1, line)
    def _(o):
        out_b(other(o)).start()

    out[rows(me), cols(me)] = back[me]

    for o in range(1, lines):
        for copy in line_copies(other_line(o), mine):
            copy.wait_send()

    @pl.loop(1, line)
    def _(o):
        q = other(o)
        out_g(q).wait_send()
        out_s(q).wait_send()
        in_b(q).wait_recv()
        out_b(q).wait_send()


def scan_states(s, g, tms):
    line = min(LINE, tms)
    lines = tms // line
    high, wide = 16, 128
    while (s.shape[0] // high) * (s.shape[1] // wide) > line:
        if wide < s.shape[1]:
            wide *= 2
        else:
            high *= 2
    f32 = jnp.float32
    return pl.pallas_call(
        functools.partial(scan_kernel, line, lines, (high, wide)),
        out_shape=jax.ShapeDtypeStruct(s.shape, s.dtype),
        in_specs=[VMEM, VMEM],
        out_specs=VMEM,
        scratch_shapes=[
            pltpu.VMEM((line, high, wide), s.dtype),
            pltpu.VMEM((line, 1, wide), f32),
            pltpu.VMEM((line, high, wide), f32),
            pltpu.VMEM((line, 1, wide), f32),
            pltpu.VMEM((line, high, wide), s.dtype),
            pltpu.VMEM((lines, high, wide), f32),
            pltpu.VMEM((lines, 1, wide), f32),
            DMA((2, line)),
            DMA((2, line)),
            DMA((2, lines)),
            DMA((2, lines)),
            DMA((2, line)),
        ],
        compiler_params=pltpu.CompilerParams(collective_id=1, has_side_effects=True),
        name="scan_states",
    )(s, g)


def mix_kernel(heads, inner, part, sq, u, w_mix, out, hid, first, full, stage, sqs, send, recv, sq_sem):
    me = lax.axis_index("head")
    right, left, across = (lax.rem(me + d, heads) for d in (1, heads - 1, 2))
    share = u.shape[0]
    half = share // 2
    width = w_mix.shape[1]
    greet([{"head": left}, {"head": right}, {"head": across}], 3)

    def halves(k):
        start = pl.multiple_of(k * share, share)
        return pl.ds(start, half), pl.ds(pl.multiple_of(start + half, half), half)

    top, bottom = pl.ds(0, half), pl.ds(half, half)
    right_top, right_bottom = halves(right)
    left_top, left_bottom = halves(left)
    across_top, across_bottom = halves(across)

    def go(n, src, dst, to):
        return remote(src, dst, send.at[n], recv.at[n], head=to)

    one = [
        go(0, part.at[across_top], first.at[0], right),
        go(1, part.at[across_bottom], first.at[1], left),
        go(2, part.at[right_bottom], full.at[0, bottom], right),
        go(3, part.at[left_top], full.at[1, top], left),
    ]
    for copy in one:
        copy.start()

    def sq_copy(to, slot):
        return remote(sq.at[to], sqs.at[slot], sq_sem.at[0, to], sq_sem.at[1, slot], head=to)

    for to in (right, left, across):
        sq_copy(to, me).start()
    sqs[me] = sq[me]
    two = [
        go(4, stage.at[0], full.at[0, top], right),
        go(5, stage.at[1], full.at[1, bottom], left),
    ]
    for n, rows in ((0, right_top), (1, left_bottom)):
        one[n].wait_recv()
        stage[n] = (part[rows].astype(jnp.float32) + first[n].astype(jnp.float32)).astype(stage.dtype)
        two[n].start()
    for frm in (right, left, across):
        sq_copy(frm, frm).wait_recv()
    square = sqs[0]
    for k in range(1, heads):
        square = square + sqs[k]
    scale = lax.rsqrt(jnp.broadcast_to(square, (share, share)).T / inner + 1e-05)
    for copy in one[2:] + two:
        copy.wait_recv()
    own = aligned(me, share)
    for k in range(u.shape[1] // share):
        cols = pl.ds(k * share, share)
        total = part[own, cols].astype(jnp.float32)
        total = total + full[0, :, cols].astype(jnp.float32) + full[1, :, cols].astype(jnp.float32)
        hid[own, cols] = (u[:, cols] + scale * total).astype(hid.dtype)
    own_top, own_bottom = halves(me)
    three = [
        go(6, hid.at[own_top], hid.at[own_top], right),
        go(7, hid.at[own_bottom], hid.at[own_bottom], left),
        go(8, hid.at[own_bottom], hid.at[own_bottom], right),
        go(9, hid.at[own_top], hid.at[own_top], left),
    ]
    for copy in three:
        copy.start()
    four = [
        go(10, hid.at[left_top], hid.at[left_top], right),
        go(11, hid.at[right_bottom], hid.at[right_bottom], left),
    ]
    mine = aligned(me, width)

    def finish(k):
        rows = aligned(k, share)
        mixed = jnp.dot(hid[rows], w_mix[...], preferred_element_type=jnp.float32)
        out[rows] = (hid[rows, mine].astype(jnp.float32) + mixed).astype(out.dtype)

    for copy, following in zip(three[:2], four):
        copy.wait_recv()
        following.start()
    finish(me)
    for copy in three[2:]:
        copy.wait_recv()
    finish(left)
    finish(right)
    for copy in four:
        copy.wait_recv()
    finish(across)
    for copy in one + two + three + four:
        copy.wait_send()
    for to in (right, left, across):
        sq_copy(to, me).wait_send()


def mix(part, sq, u, w_mix, heads, inner):
    rows, width = part.shape
    share = rows // heads
    bf16 = jnp.bfloat16
    return pl.pallas_call(
        functools.partial(mix_kernel, heads, inner),
        out_shape=jax.ShapeDtypeStruct((rows, w_mix.shape[1]), bf16),
        in_specs=[VMEM] * 4,
        out_specs=VMEM,
        scratch_shapes=[
            pltpu.VMEM((rows, width), bf16),
            pltpu.VMEM((2, share // 2, width), bf16),
            pltpu.VMEM((2, share, width), bf16),
            pltpu.VMEM((2, share // 2, width), bf16),
            pltpu.VMEM((heads, 1, share), jnp.float32),
            DMA((12,)),
            DMA((12,)),
            DMA((2, heads)),
        ],
        compiler_params=pltpu.CompilerParams(collective_id=2, has_side_effects=True),
        name="mix_rows",
    )(part, sq, u, w_mix)


def sinusoid(timestep, width):
    half = width // 2
    freq = jnp.exp(-math.log(10000.0) * jnp.arange(half, dtype=jnp.float32) / half)
    angle = timestep.astype(jnp.float32)[0] * freq
    return jnp.concatenate([jnp.sin(angle), jnp.cos(angle)])


def causal_conv(rows, kernel):
    width = kernel.shape[0]
    count = rows.shape[0] - RIM
    first = RIM - width + 1
    total = jnp.zeros((count, rows.shape[1]), jnp.float32)
    for k in range(width):
        total = total + rows[first + k : first + k + count].astype(jnp.float32) * kernel[k]
    return jax.nn.silu(total).astype(jnp.bfloat16)


def spread(per_head, hdim):
    return jnp.repeat(per_head, hdim, axis=-1)


def diagonal(xa, bmat, cmat, dt, cum):
    steps = xa.shape[0]
    scores = jnp.dot(cmat, bmat.T, preferred_element_type=jnp.float32)
    rowid = lax.broadcasted_iota(jnp.int32, (steps, steps), 0)
    colid = lax.broadcasted_iota(jnp.int32, (steps, steps), 1)
    causal = rowid >= colid
    cumt = cum.T
    seg = cumt[:, :, None] - cumt[:, None, :]
    decay = jnp.exp(jnp.where(causal[None], seg, -jnp.inf))
    mixw = (scores[None] * decay * dt.T[:, None, :]).astype(jnp.bfloat16)
    return jnp.einsum("hij,jhp->ihp", mixw, xa, preferred_element_type=jnp.float32)


def shards(
    latent,
    timestep,
    in_gain,
    w_x,
    w_z,
    w_bc,
    w_dt,
    conv_x,
    conv_bc,
    dt_bias,
    a_log,
    d_skip,
    norm_gain,
    w_out,
    w_mix,
):
    f32, bf16 = jnp.float32, jnp.bfloat16
    tms, devices = lax.axis_size("tm"), lax.axis_size("head")
    whole = gather(latent, tms, devices)
    emb = sinusoid(timestep, whole.shape[1])[None, :]
    u = whole.astype(f32) + emb
    normed = (u * lax.rsqrt(jnp.mean(u * u, axis=1, keepdims=True) + 1e-05) * in_gain).astype(bf16)
    xs = jnp.dot(normed, w_x, preferred_element_type=f32).astype(bf16)
    bc = jnp.dot(normed, w_bc, preferred_element_type=f32).astype(bf16)
    gate = jnp.dot(normed[RIM:], w_z, preferred_element_type=f32).astype(bf16)
    dt_raw = jnp.dot(normed[RIM:], w_dt, preferred_element_type=f32)
    inside = (lax.broadcasted_iota(jnp.int32, (xs.shape[0], 1), 0) >= RIM) | (lax.axis_index("tm") > 0)
    xa = causal_conv(jnp.where(inside, xs, 0), conv_x)
    bca = causal_conv(jnp.where(inside, bc, 0), conv_bc)
    state_n = w_bc.shape[1] // 2
    dt = jax.nn.softplus(dt_raw + dt_bias)
    la = dt * -jnp.exp(a_log)
    steps, heads = dt.shape
    hdim = xa.shape[1] // heads
    blocks = steps // BLOCK
    terms = []
    for b in range(blocks):
        rows = slice(b * BLOCK, (b + 1) * BLOCK)
        bmat, cmat = bca[rows, :state_n], bca[rows, state_n:]
        cum = jnp.cumsum(la[rows], axis=0)
        tail = jnp.exp(cum[-1:] - cum) * dt[rows]
        weighted = (xa[rows].astype(f32) * spread(tail, hdim)).astype(bf16)
        state = lax.dot_general(
            bmat, weighted, (((0,), (0,)), ((), ())), preferred_element_type=f32
        )
        total = spread(jnp.exp(cum[-1:]), hdim)
        terms.append((rows, bmat, cmat, cum, state, total))
    run_state, run_total = terms[0][4], terms[0][5]
    for term in terms[1:]:
        run_state, run_total = run_state * term[5] + term[4], run_total * term[5]
    incoming = scan_states(run_state.astype(bf16), run_total, tms).astype(f32)
    ys = []
    for rows, bmat, cmat, cum, state, total in terms:
        ydiag = diagonal(xa[rows].reshape(BLOCK, heads, hdim), bmat, cmat, dt[rows], cum)
        yoff = jnp.dot(cmat, incoming.astype(bf16), preferred_element_type=f32)
        ys.append(ydiag.reshape(BLOCK, heads * hdim) + yoff * spread(jnp.exp(cum), hdim))
        incoming = incoming * total + state
    y = jnp.concatenate(ys, axis=0) + spread(d_skip[None, :], hdim) * xa.astype(f32)
    gated = y * jax.nn.silu(gate.astype(f32))
    share = steps // devices
    square = jnp.sum(gated * gated, axis=1).reshape(devices, 1, share)
    scaled = (gated * norm_gain).astype(bf16)
    part = jnp.dot(scaled, w_out, preferred_element_type=f32).astype(bf16)
    own = lax.dynamic_slice_in_dim(whole, RIM + lax.axis_index("head") * share, share, 0)
    inner = gated.shape[1] * devices
    return mix(part, square, own.astype(f32) + emb, w_mix, devices, inner)


def solution(mesh):
    in_specs = (
        P("tm", "head"),
        P(),
        P(),
        P(None, "head"),
        P(None, "head"),
        P(),
        P(None, "head"),
        P(None, "head"),
        P(),
        P("head"),
        P("head"),
        P("head"),
        P("head"),
        P("head", None),
        P(None, "head"),
    )
    out_specs = P("tm", "head")
    return jax.shard_map(shards, mesh=mesh, in_specs=in_specs, out_specs=out_specs, check_vma=False)
```

time: 533 us -> 141 us (0.26)
  waiting for transfers between devices: 380 us -> 0 us
  Pallas kernels: 0 us -> 88.2 us
  blocking collectives: 87.4 us -> 0 us
  between operations: 14.1 us -> 1.04 us
  local copies, waits for them, and re-layouts: 9.3 us -> 21.2 us
  starting transfers between devices: 7.41 us -> 0 us
    reduce_scatter x1 -> x0, waiting for transfers between devices: 199 us -> none  [shards(): lax.psum_scatter(jnp.dot(yn, w_out, preferred_element_type=jnp.float32),...]
    all_gather x3 -> x0, waiting for transfers between devices: 181 us -> none  [the longest x1 116 us: prefix(): gathered = jax.tree.map(lambda a: lax.all_gather(a, axis), part)]
    pallas_call x0 -> x3, Pallas kernels: none -> 88.2 us  [the longest x1 44.7 us: scan_states(): pl.pallas_call(functools.partial(scan_kernel, line, lines, (high, wide)),...]
    all_gather x1 -> x0, blocking collectives: 78.9 us -> none  [prefix(): gathered = jax.tree.map(lambda a: lax.all_gather(a, axis), part)]
    psum x1 -> x0, blocking collectives: 8.46 us -> none  [shards(): square = lax.psum(jnp.sum(gated * gated, axis=1), 'head')]
    ppermute x2 -> x0, starting transfers between devices: 7.25 us -> none  [from_behind(): return lax.ppermute(block, axis, route)]
    reshape x4 -> x7, local copies, waits for them, and re-layouts: 4.61 us -> 10.2 us  [the longest x4 7.14 us: spread(): return jnp.repeat(per_head, hdim, axis=-1)]
    dot_general x9 -> x13, matrix products: 16.2 us -> 21.5 us  [the longest x2 4.47 us: shards(): yoff = jnp.dot(cmat, incoming.astype(bf16), preferred_element_type=f32)]
  transfers between devices with their start and end apart: 6 -> 0, of which waited for: 4 -> 0; matrix products, arithmetic and copies ran while one was open for 1% -> 0% of each run, Pallas kernels for 0% -> 0%
where the time goes in v1:
time: 141 us; the launch traced here: 140 us
  Pallas kernels  88.2 us (63%)
  matrix products  21.5 us (15%)
  local copies, waits for them, and re-layouts  21.2 us (15%)
  other arithmetic  8.04 us (6%)
    pallas_call x1, Pallas kernels, scan_states(): pl.pallas_call(functools.partial(scan_kernel, line, lines, (high, wide)),...  44.7 us
    pallas_call x1, Pallas kernels, mix(): pl.pallas_call(functools.partial(mix_kernel, heads, inner), out_shape=jax...  25.4 us
    pallas_call x1, Pallas kernels, gather(): pl.pallas_call(functools.partial(gather_kernel, tms, heads), out_shape=ja...  18 us
    reshape x4, local copies, waits for them, and re-layouts, spread(): return jnp.repeat(per_head, hdim, axis=-1)  7.14 us
    dot_general x2, matrix products, shards(): yoff = jnp.dot(cmat, incoming.astype(bf16), preferred_element_type=f32)  4.47 us
    dot_general x2, matrix products, diagonal(): jnp.einsum('hij,jhp->ihp', mixw, xa, preferred_element_type=jnp.float32)  4.31 us
    dot_general x1, matrix products, shards(): gate = jnp.dot(normed[RIM:], w_z, preferred_element_type=f32).astype(bf16)  3.44 us
    dot_general x2, matrix products, shards(): lax.dot_general(bmat, weighted, (((0,), (0,)), ((), ())), preferred_eleme...  3.16 us

profile of v1, /device:TPU:1, one launch (start us, length us, event | category | flops | bytes accessed | tf_op | source)
XLA Modules:
  0.0 140.0 jit_solution(5302950261611046454)
XLA Ops:
  0.8 18.0 %gather_rows.1 = bf16[528,1024]{1,0:T(8,128)(2,1)} custom-call(bf16[512,256]{1,0:T(8,128)(2,1)} %lat.1), custom_call_target="tpu_custom_call" | custom-call | tf_op jit(solution)/shard_map/gather_rows/pallas_call | solution.py:104
  18.8 1.7 %multiply_reduce_fusion = f32[528]{0:T(1024)S(1)} fusion(bf16[528,1024]{1,0:T(8,128)(2,1)} %gather_rows.1, f32[1024]{0:T(1024)S(1)} %pad_maximum_fusion), kind=kLoop, calls=%fused_computation.1 | loop fusion | flops 2162160 | bytes 1087552 | tf_op jit(solution)/shard_map/reduce_sum | solution.py:448
  23.2 0.8 exponential_reduce_fusion.1
  25.4 0.7 exponential_reduce_fusion
  27.5 1.5 %fusion.3 = bf16[528,256]{1,0:T(8,128)(2,1)S(1)} fusion(bf16[528,1024]{1,0:T(8,128)(2,1)S(1)} %multiply_convert_fusion, bf16[1024,256]{1,0:T(8,128)(2,1)} %param.20, pred[528]{0:T(1024)(128)(4,1)S(1)} %fusion.40), kind=kOutput, calls=%fused_computation.16 | convolution fusion | flops 277094400 | bytes 1876496 | tf_op jit(solution)/shard_map/dot_general | solution.py:450
  29.4 0.9 fusion.34
  30.3 0.7 fusion
  31.7 0.7 fusion.49
  32.5 0.9 copy.25
  33.4 1.8 %fusion.5 = f32[8,64,256]{2,1,0:T(8,128)S(1)} fusion(bf16[256,8,64]{0,2,1:T(8,128)(2,1)} %bitcast.62, f32[8,256]{1,0:T(8,128)S(1)} %copy-done.11, f32[8,256]{1,0:T(8,128)S(1)} %copy-done.9, f32[256,256]{1,0:T(8,128)} %fusion.34, pred[256,256]{1,0:T(8,128)(4,1)S(1)} %iota_compare_fusion), kind=kOutput, calls=%fused_computation.20 | convolution fusion | flops 69730304 | bytes 1130496 | tf_op jit(solution)/shard_map/hij,jhp->ihp/dot_general | solution.py:423
  35.1 1.0 copy.29
  36.2 1.0 copy.26
  37.2 1.2 fusion.26
  38.5 0.8 broadcast_in_dim.97
  39.3 2.1 %copy.27 = f32[256,512]{1,0:T(8,128)} copy(f32[256,512]{0,1:T(8,128)} %bitcast.57) | data formatting | bytes 1048576 | tf_op jit(solution)/shard_map/reshape | solution.py:410
  41.5 1.9 %fusion.4.s = bf16[128,512]{1,0:T(8,128)(2,1)} fusion(f32[256,512]{1,0:T(8,128)} %copy.27, f32[128,512]{1,0:T(8,128)S(1)} %fusion.26, f32[512]{0:T(512)S(1)} %broadcast_in_dim.96, bf16[512,256]{1,0:T(8,128)(2,1)S(1)} %multiply_convert_fusion.10, bf16[512,512]{1,0:T(8,128)(2,1)S(1)} %multiply_convert_fusion.6), kind=kOutput, calls=%fused_computation.18 | convolution fusion | flops 34144256 | bytes 1247232 | tf_op jit(solution)/shard_map/dot_general | solution.py:469
  44.2 44.7 %scan_states.1 = bf16[128,512]{1,0:T(8,128)(2,1)} custom-call(bf16[128,512]{1,0:T(8,128)(2,1)} %fusion.4.s, f32[1,512]{1,0:T(1,128)} %mul.268.g), custom_call_target="tpu_custom_call" | custom-call | tf_op jit(solution)/shard_map/scan_states/pallas_call | solution.py:250
  89.0 0.8 broadcast_in_dim.99
  89.8 2.0 %copy.28 = f32[256,512]{1,0:T(8,128)} copy(f32[256,512]{0,1:T(8,128)} %bitcast.58) | data formatting | bytes 1048576 | tf_op jit(solution)/shard_map/reshape | solution.py:410
  91.8 2.2 %fusion.1 = f32[256,512]{1,0:T(8,128)} fusion(f32[256,512]{1,0:T(8,128)} %copy.29, f32[256,512]{1,0:T(8,128)} %copy.28, bf16[128,512]{1,0:T(8,128)(2,1)S(1)} %copy-done.2, bf16[512,256]{1,0:T(8,128)(2,1)S(1)} %multiply_convert_fusion.10), kind=kOutput, calls=%fused_computation.13 | convolution fusion | flops 33816576 | bytes 1769472 | tf_op jit(solution)/shard_map/dot_general | solution.py:481
  94.1 0.9 fusion.29
  95.0 1.8 %copy.30 = bf16[256,512]{0,1:T(8,128)(2,1)} copy(bf16[256,512]{1,0:T(8,128)(2,1)} %get-tuple-element.14) | data formatting | bytes 524288 | tf_op jit(solution)/shard_map/slice | solution.py:468
  96.8 2.6 %fusion.6 = f32[8,64,256]{2,1,0:T(8,128)} fusion(bf16[256,8,64]{0,2,1:T(8,128)(2,1)} %bitcast.63, f32[8,256]{1,0:T(8,128)S(1)} %copy-done.10, f32[8,256]{1,0:T(8,128)S(1)} %add_bitcast_fusion.1, f32[256,256]{1,0:T(8,128)} %fusion.29, pred[256,256]{1,0:T(8,128)(4,1)S(1)} %iota_compare_fusion), kind=kOutput, calls=%fused_computation.21 | convolution fusion | flops 69730304 | bytes 1130496 | tf_op jit(solution)/shard_map/hij,jhp->ihp/dot_general | solution.py:423
  99.4 2.0 %copy.32 = f32[256,512]{1,0:T(8,128)} copy(f32[256,512]{0,1:T(8,128)} %bitcast.60) | data formatting | bytes 1048576 | tf_op jit(solution)/shard_map/reshape | solution.py:482
  101.6 0.8 broadcast_in_dim.102
  102.4 2.0 %copy.31 = f32[256,512]{1,0:T(8,128)} copy(f32[256,512]{0,1:T(8,128)} %bitcast.59) | data formatting | bytes 1048576 | tf_op jit(solution)/shard_map/reshape | solution.py:410
  104.5 2.2 %fusion.2 = f32[256,512]{1,0:T(8,128)} fusion(f32[256,512]{1,0:T(8,128)} %copy.32, f32[256,512]{1,0:T(8,128)} %copy.31, f32[128,512]{1,0:T(8,128)S(1)} %fusion.26, bf16[128,512]{1,0:T(8,128)(2,1)S(1)} %copy-done.2, f32[512]{0:T(512)S(1)} %broadcast_in_dim.101, bf16[512,256]{1,0:T(8,128)(2,1)S(1)} %multiply_convert_fusion.10), kind=kOutput, calls=%fused_computation.14 | convolution fusion | flops 34078720 | bytes 2033664 | tf_op jit(solution)/shard_map/dot_general | solution.py:481
  106.9 3.4 %multiply_reduce_fusion.1 = (f32[512]{0:T(512)}, f32[512,512]{1,0:T(8,128)S(1)}) fusion(bf16[1024,512]{1,0:T(8,128)(2,1)} %param.19, bf16[528,1024]{1,0:T(8,128)(2,1)} %copy-done.3, bf16[512,512]{1,0:T(8,128)(2,1)S(1)} %multiply_convert_fusion.6, f32[512]{0:T(512)S(1)} %broadcast_in_dim.104, f32[256,512]{1,0:T(8,128)} %fusion.2, f32[256,512]{1,0:T(8,128)} %fusion.1), kind=kOutput, calls=%fused_computation.27 | convolution fusion | flops 540278272 | bytes 4722688 | tf_op jit(solution)/shard_map/dot_general | solution.py:451
  110.3 1.7 %convolution_convert_fusion.part = bf16[512,1024]{1,0:T(8,128)(2,1)} fusion(bf16[512,1024]{1,0:T(8,128)(2,1)S(1)} %copy-done, f32[512,512]{1,0:T(8,128)S(1)} %get-tuple-element.32, f32[512]{0:T(512)S(1)} %copy-done.16), kind=kOutput, calls=%fused_computation.5 | convolution fusion | flops 537919488 | bytes 3147776 | tf_op jit(solution)/shard_map/dot_general | solution.py:489
  112.0 0.9 convert_add_fusion.1.u
  112.9 25.4 %mix_rows.1 = bf16[512,256]{1,0:T(8,128)(2,1)} custom-call(bf16[512,1024]{1,0:T(8,128)(2,1)} %convolution_convert_fusion.part, f32[4,1,128]{2,1,0:T(1,128)} %bitcast.72, f32[128,1024]{1,0:T(8,128)} %convert_add_fusion.1.u, bf16[1024,256]{1,0:T(8,128)(2,1)} %w_mix.1), custom_call_target="tpu_custom_call" | custom-call | tf_op jit(solution)/shard_map/mix_rows/pallas_call | solution.py:372
  138.3 1.7 %copy.37 = bf16[512,256]{1,0:T(8,128)(2,1)} copy(bf16[512,256]{1,0:T(8,128)(2,1)} %mix_rows.1) | data formatting | bytes 524288
  (80 shorter events, 7.9 us)
Async XLA Ops:
  0.0 110.3 %copy-start = (bf16[512,1024]{1,0:T(8,128)(2,1)S(1)}, bf16[512,1024]{1,0:T(8,128)(2,1)}, u32[]{:S(2)}) copy-start(bf16[512,1024]{1,0:T(8,128)(2,1)} %param.28) | copy-start | bytes 3145732
  0.8 19.7 %copy-start.12 = (f32[1024]{0:T(1024)S(1)}, f32[1024]{0:T(1024)}, u32[]{:S(2)}) copy-start(f32[1024]{0:T(1024)} %param.17) | copy-start | bytes 12292
  18.8 1.7 %copy-start.1 = (bf16[528,1024]{1,0:T(8,128)(2,1)S(1)}, bf16[528,1024]{1,0:T(8,128)(2,1)}, u32[]{:S(2)}) copy-start(bf16[528,1024]{1,0:T(8,128)(2,1)} %gather_rows.1) | copy-start | bytes 3244036
  20.6 0.7 copy-start.20
  20.6 0.7 copy-start.19
  20.6 0.7 copy-start.21
  21.2 9.0 %copy-start.3 = (bf16[528,1024]{1,0:T(8,128)(2,1)}, bf16[528,1024]{1,0:T(8,128)(2,1)S(1)}, u32[]{:S(2)}) copy-start(bf16[528,1024]{1,0:T(8,128)(2,1)S(1)} %multiply_convert_fusion) | copy-start | bytes 3244036
  27.5 1.5 %copy-start.13 = (f32[4,256]{1,0:T(4,128)S(1)}, f32[4,256]{1,0:T(4,128)}, u32[]{:S(2)}) copy-start(f32[4,256]{1,0:T(4,128)} %param.23) | copy-start | bytes 12292
  29.0 1.3 copy-start.18
  30.3 0.7 copy-start.8
  31.7 1.6 %copy-start.9 = (f32[8,256]{1,0:T(8,128)S(1)}, f32[8,256]{1,0:T(8,128)}, u32[]{:S(2)}) copy-start(f32[8,256]{1,0:T(8,128)} %add_bitcast_fusion.3) | copy-start | bytes 24580
  31.7 1.6 %copy-start.11 = (f32[8,256]{1,0:T(8,128)S(1)}, f32[8,256]{1,0:T(8,128)}, u32[]{:S(2)}) copy-start(f32[8,256]{1,0:T(8,128)} %get-tuple-element.15) | copy-start | bytes 24580
  33.4 2.8 %copy-start.7 = (f32[256,8]{0,1:T(8,128)S(1)}, f32[256,8]{0,1:T(8,128)}, u32[]{:S(2)}) copy-start(f32[256,8]{0,1:T(8,128)} %get-tuple-element.16) | copy-start | bytes 24580
  36.2 2.3 %copy-start.6 = (f32[256,8]{0,1:T(8,128)S(1)}, f32[256,8]{0,1:T(8,128)}, u32[]{:S(2)}) copy-start(f32[256,8]{0,1:T(8,128)} %get-tuple-element.18) | copy-start | bytes 24580
  37.2 4.2 %copy-start.15 = (f32[8]{0:T(128)S(1)}, f32[8]{0:T(128)}, u32[]{:S(2)}) copy-start(f32[8]{0:T(128)} %get-tuple-element.7) | copy-start | bytes 100
  39.3 4.1 %copy-start.14 = (f32[8]{0:T(128)S(1)}, f32[8]{0:T(128)}, u32[]{:S(2)}) copy-start(f32[8]{0:T(128)} %get-tuple-element.5) | copy-start | bytes 100
  39.3 49.6 %copy-start.5 = (f32[256,8]{0,1:T(8,128)S(1)}, f32[256,8]{0,1:T(8,128)}, u32[]{:S(2)}) copy-start(f32[256,8]{0,1:T(8,128)} %get-tuple-element.9) | copy-start | bytes 24580
  88.9 2.9 %copy-start.2 = (bf16[128,512]{1,0:T(8,128)(2,1)S(1)}, bf16[128,512]{1,0:T(8,128)(2,1)}, u32[]{:S(2)}) copy-start(bf16[128,512]{1,0:T(8,128)(2,1)} %scan_states.1) | copy-start | bytes 393220
  91.8 5.0 %copy-start.10 = (f32[8,256]{1,0:T(8,128)S(1)}, f32[8,256]{1,0:T(8,128)}, u32[]{:S(2)}) copy-start(f32[8,256]{1,0:T(8,128)} %get-tuple-element.17) | copy-start | bytes 24580
  96.8 4.8 %copy-start.4 = (f32[256,8]{0,1:T(8,128)S(1)}, f32[256,8]{0,1:T(8,128)}, u32[]{:S(2)}) copy-start(f32[256,8]{0,1:T(8,128)} %get-tuple-element.11) | copy-start | bytes 24580
  104.5 2.3 %copy-start.17 = (f32[8]{0:T(128)S(1)}, f32[8]{0:T(128)}, u32[]{:S(2)}) copy-start(f32[8]{0:T(128)} %param.26) | copy-start | bytes 100
  106.9 3.4 %copy-start.16 = (f32[512]{0:T(512)S(1)}, f32[512]{0:T(512)}, u32[]{:S(2)}) copy-start(f32[512]{0:T(512)} %param.27) | copy-start | bytes 6148

commit v2 on v1

v2 whole, which is shorter than its diff:
```python
import functools
import math

import jax
import jax.numpy as jnp
from jax import lax
from jax.experimental import pallas as pl
from jax.experimental.pallas import tpu as pltpu
from jax.sharding import PartitionSpec as P

BLOCK = 256
RIM = 16
LINE = 32
MESH = pl.DeviceIdType.MESH
VMEM = pl.BlockSpec(memory_space=pltpu.VMEM)
DMA = pltpu.SemaphoreType.DMA


def remote(src, dst, send, recv, **device):
    return pltpu.make_async_remote_copy(
        src_ref=src, dst_ref=dst, send_sem=send, recv_sem=recv, device_id=device, device_id_type=MESH
    )


def greet(devices, count):
    barrier = pltpu.get_barrier_semaphore()
    for device in devices:
        pl.semaphore_signal(barrier, inc=1, device_id=device, device_id_type=MESH)
    pl.semaphore_wait(barrier, count)


def aligned(index, size):
    return pl.ds(pl.multiple_of(index * size, size), size)


def gather_kernel(tms, heads, lat, out, own_sem, send, recv, rim_send, rim_recv):
    tm, me = lax.axis_index("tm"), lax.axis_index("head")
    right, left = lax.rem(me + 1, heads), lax.rem(me + heads - 1, heads)
    later, earlier = lax.rem(tm + 1, tms), lax.rem(tm + tms - 1, tms)
    rows, width = lat.shape
    half = rows // 2
    greet(
        [{"head": left}, {"head": right}] + [{"tm": earlier, "head": h} for h in range(heads)],
        2 + heads,
    )
    top, bottom = pl.ds(RIM, half), pl.ds(RIM + half, half)
    mine, lefts, rights = aligned(me, width), aligned(left, width), aligned(right, width)

    def own(rows_out, start, sem, to):
        return remote(
            lat.at[pl.ds(start, half)], out.at[rows_out, mine], send.at[sem], recv.at[sem], head=to
        )

    copies = [
        own(top, 0, 0, right),
        own(bottom, half, 1, left),
        own(bottom, half, 2, right),
        own(top, 0, 3, left),
    ]
    for copy in copies[:2]:
        copy.start()
    rims = [
        remote(
            lat.at[pl.ds(rows - RIM, RIM)],
            out.at[pl.ds(0, RIM), mine],
            rim_send.at[h],
            rim_recv.at[me],
            tm=later,
            head=h,
        )
        for h in range(heads)
    ]
    for copy in rims:
        copy.start()
    for copy in copies[2:]:
        copy.start()
    keep = pltpu.make_async_copy(lat, out.at[pl.ds(RIM, rows), mine], own_sem)
    keep.start()
    onward = [
        remote(out.at[top, lefts], out.at[top, lefts], send.at[4], recv.at[4], head=right),
        remote(out.at[bottom, rights], out.at[bottom, rights], send.at[5], recv.at[5], head=left),
    ]
    for copy, following in zip(copies[:2], onward):
        copy.wait_recv()
        following.start()
    for copy in copies[2:] + onward:
        copy.wait_recv()
    for h in range(heads):
        remote(
            lat.at[pl.ds(rows - RIM, RIM)],
            out.at[pl.ds(0, RIM), pl.ds(h * width, width)],
            rim_send.at[h],
            rim_recv.at[h],
            tm=later,
            head=h,
        ).wait_recv()
    for copy in copies + onward + rims:
        copy.wait_send()
    keep.wait()


def gather(lat, tms, heads):
    rows, width = lat.shape
    return pl.pallas_call(
        functools.partial(gather_kernel, tms, heads),
        out_shape=jax.ShapeDtypeStruct((rows + RIM, width * heads), lat.dtype),
        in_specs=[VMEM],
        out_specs=VMEM,
        scratch_shapes=[DMA, DMA((6,)), DMA((6,)), DMA((heads,)), DMA((heads,))],
        compiler_params=pltpu.CompilerParams(collective_id=0, has_side_effects=True),
        name="gather_rows",
    )(lat)


def split(value):
    parts = []
    for _ in range(3):
        part = value.astype(jnp.bfloat16)
        parts.append(part)
        value = value - part.astype(jnp.float32)
    return parts


def exact(value, ones):
    total = None
    for part in split(value):
        term = jnp.dot(part, ones, preferred_element_type=jnp.float32)
        total = term if total is None else total + term
    return total


def iota(shape, axis):
    return lax.broadcasted_iota(jnp.int32, shape, axis)


def column(row):
    count = row.shape[1]
    wide = jnp.broadcast_to(row, (count, count))
    return jnp.sum(
        jnp.where(iota((count, count), 0) == iota((count, count), 1), wide, 0.0), axis=1, keepdims=True
    )


def layer_kernel(
    tms,
    line,
    piece,
    devices,
    whole,
    emb,
    in_gain,
    w_x,
    w_z,
    w_bc,
    w_dt,
    conv_x,
    conv_bc,
    dt_bias,
    a_log,
    d_skip,
    norm_gain,
    w_out,
    w_mix,
    out,
    nrm,
    xs,
    bcs,
    xa,
    bb,
    cc,
    cums,
    dts,
    cols_t,
    ec,
    states,
    totals,
    s,
    g,
    yd,
    z,
    hin,
    hb,
    part,
    sq,
    sin,
    gin,
    pre,
    dec,
    back,
    xt,
    xd,
    hid,
    first,
    full,
    stage,
    sqs,
    s_sem,
    g_sem,
    xt_sem,
    xd_sem,
    b_sem,
    send,
    recv,
    sq_sem,
):
    f32, bf16 = jnp.float32, jnp.bfloat16
    lines = tms // line
    tm = lax.axis_index("tm")
    here, mine = lax.rem(tm, line), tm // line
    base = mine * line
    high, wide = piece
    stack = s.shape[0] // high
    me = lax.axis_index("head")
    right, left, across = (lax.rem(me + d, devices) for d in (1, devices - 1, 2))

    def rows(k):
        return aligned(lax.rem(k, stack), high)

    def cols(k):
        return aligned(k // stack, wide)

    def other(o):
        return lax.rem(here + o, line)

    def other_line(o):
        return lax.rem(mine + o, lines)

    barrier = pltpu.get_barrier_semaphore()

    @pl.loop(1, line)
    def _(o):
        pl.semaphore_signal(barrier, inc=1, device_id={"tm": base + other(o)}, device_id_type=MESH)

    for o in range(1, lines):
        pl.semaphore_signal(
            barrier, inc=1, device_id={"tm": other_line(o) * line + here}, device_id_type=MESH
        )
    for device in (left, right, across):
        pl.semaphore_signal(barrier, inc=1, device_id={"head": device}, device_id_type=MESH)

    total_rows = whole.shape[0]
    steps = total_rows - RIM
    chunk = total_rows // 11

    @pl.loop(0, 11)
    def _(c):
        at = aligned(c, chunk)
        u = whole[at].astype(f32) + emb[...]
        mean = jnp.mean(u * u, axis=1, keepdims=True)
        nrm[at] = (u * lax.rsqrt(mean + 1e-05) * in_gain[...]).astype(bf16)

    dt_t = lax.dot_general(
        w_dt[...], nrm[RIM:], (((1,), (1,)), ((), ())), preferred_element_type=f32
    )
    xs[...] = jnp.dot(nrm[...], w_x[...], preferred_element_type=f32).astype(bf16).astype(f32)
    bcs[...] = jnp.dot(nrm[...], w_bc[...], preferred_element_type=f32).astype(bf16).astype(f32)

    @pl.when(tm == 0)
    def _():
        xs[:RIM] = jnp.zeros((RIM, xs.shape[1]), f32)
        bcs[:RIM] = jnp.zeros((RIM, bcs.shape[1]), f32)

    taps = conv_x.shape[0]
    state_n = bb.shape[1]
    width = 128

    def conv(source, kernel, c, lanes):
        value = source[pl.ds(pl.multiple_of(c * width + RIM - 8, 8), width + 8), lanes]
        total = jnp.zeros((width, value.shape[1]), f32)
        for k in range(taps):
            at = 8 - taps + 1 + k
            total = total + value[at : at + width] * kernel[k : k + 1, lanes]
        return jax.nn.silu(total).astype(bf16)

    @pl.loop(0, steps // width)
    def _(c):
        at = aligned(c, width)
        for lane in range(0, xs.shape[1], 128):
            lanes = pl.ds(lane, 128)
            xa[at, lanes] = conv(xs, conv_x, c, lanes)
        bb[at] = conv(bcs, conv_bc, c, pl.ds(0, state_n))
        cc[at] = conv(bcs, conv_bc, c, pl.ds(state_n, state_n))

    raw = dt_t + column(dt_bias[...])
    dt_t = jnp.maximum(raw, 0.0) + jnp.log1p(jnp.exp(-jnp.abs(raw)))
    la_t = dt_t * -jnp.exp(column(a_log[...]))
    heads = dt_t.shape[0]
    channels = xa.shape[1]
    hdim = channels // heads
    blocks = steps // BLOCK
    upper = jnp.where(iota((BLOCK, BLOCK), 0) <= iota((BLOCK, BLOCK), 1), 1.0, 0.0).astype(bf16)

    def picks(offset):
        hit = iota((128, channels), 0) == iota((128, channels), 1) // hdim + offset
        return jnp.where(hit, 1.0, 0.0).astype(bf16)

    tail_picks, decay_picks = picks(heads), picks(2 * heads)
    for b in range(blocks):
        span = slice(b * BLOCK, (b + 1) * BLOCK)
        dt_b = dt_t[:, span]
        cum_b = exact(la_t[:, span], upper)
        last = cum_b[:, BLOCK - 1 :]
        tail = jnp.exp(last - cum_b) * dt_b
        cums[b] = cum_b
        dts[b] = dt_b
        pad = jnp.zeros((128 - 3 * heads, BLOCK), f32)
        columns = jnp.concatenate([cum_b, tail, jnp.exp(cum_b), pad], axis=0).T
        cols_t[span] = columns
        ec[span] = exact(columns, decay_picks)
        weighted = (xa[span].astype(f32) * exact(columns, tail_picks)).astype(bf16)
        states[b] = jnp.dot(
            bb[span].astype(f32).T.astype(bf16), weighted, preferred_element_type=f32
        )
        totals[b] = ec[(b + 1) * BLOCK - 1 : (b + 1) * BLOCK]
    run_state, run_total = states[0], totals[0]
    for b in range(1, blocks):
        run_state, run_total = run_state * totals[b] + states[b], run_total * totals[b]
    s[...] = run_state.astype(bf16)
    g[...] = run_total
    pl.semaphore_wait(barrier, line - 1 + lines - 1 + 3)

    def out_s(q):
        return remote(s.at[rows(q), cols(q)], sin.at[here], s_sem.at[0, q], s_sem.at[1, here], tm=base + q)

    def out_g(q):
        return remote(g.at[:, cols(q)], gin.at[here], g_sem.at[0, q], g_sem.at[1, here], tm=base + q)

    def in_s(q):
        return remote(s.at[rows(q), cols(q)], sin.at[q], s_sem.at[0, q], s_sem.at[1, q], tm=base + q)

    def in_g(q):
        return remote(g.at[:, cols(q)], gin.at[q], g_sem.at[0, q], g_sem.at[1, q], tm=base + q)

    @pl.loop(1, line)
    def _(o):
        q = other(o)
        out_g(q).start()
        out_s(q).start()

    sin[here] = s[rows(here), cols(here)]
    gin[here] = g[:, cols(here)]

    def diagonal(b):
        at = aligned(b, BLOCK)
        scores = lax.dot_general(
            cc[at], bb[at], (((1,), (1,)), ((), ())), preferred_element_type=f32
        )
        causal = iota((BLOCK, BLOCK), 0) >= iota((BLOCK, BLOCK), 1)
        cols_b, cum_b, dt_b = cols_t[at], cums[b], dts[b]
        per = 128 // hdim
        for first_head in range(0, heads, per):
            lanes = slice(first_head * hdim, (first_head + per) * hdim)
            xa_b = xa[at, lanes]
            lane = iota((BLOCK, 128), 1) // hdim
            total = jnp.zeros((BLOCK, 128), f32)
            for i in range(per):
                h = first_head + i
                seg = jnp.where(causal, cols_b[:, h : h + 1] - cum_b[h : h + 1], -jnp.inf)
                mixw = (scores * jnp.exp(seg) * dt_b[h : h + 1]).astype(bf16)
                product = jnp.dot(mixw, xa_b, preferred_element_type=f32)
                total = jnp.where(lane == i, product, total)
            yd[at, lanes] = total

    diagonal(0)

    def step(k, carry):
        state, decay = carry

        @pl.when(k != here)
        def _():
            in_g(k).wait_recv()
            in_s(k).wait_recv()

        pre[k] = state
        dec[k] = decay
        factor = gin[k]
        return state * factor + sin[k].astype(f32), decay * factor

    state, decay = lax.fori_loop(
        0, line, step, (jnp.zeros((high, wide), f32), jnp.ones((1, wide), f32))
    )
    xt[mine] = state
    xd[mine] = decay

    def line_copies(q, slot):
        device = q * line + here
        return (
            remote(xt.at[slot], xt.at[slot], xt_sem.at[0, q], xt_sem.at[1, slot], tm=device),
            remote(xd.at[slot], xd.at[slot], xd_sem.at[0, q], xd_sem.at[1, slot], tm=device),
        )

    for o in range(1, lines):
        for copy in line_copies(other_line(o), mine):
            copy.start()
    z[...] = jax.nn.silu(
        jnp.dot(nrm[RIM:], w_z[...], preferred_element_type=f32).astype(bf16).astype(f32)
    )
    for o in range(1, lines):
        for copy in line_copies(other_line(o), other_line(o)):
            copy.wait_recv()
    start = jnp.zeros((high, wide), f32)
    for k in range(lines):
        start = jnp.where(k < mine, start * xd[k] + xt[k], start)

    def final(k, carry):
        back[k] = (start * dec[k] + pre[k]).astype(back.dtype)
        return carry

    lax.fori_loop(0, line, final, 0)

    def out_b(q):
        return remote(
            back.at[q], hin.at[rows(here), cols(here)], b_sem.at[0, q], b_sem.at[1, here], tm=base + q
        )

    def in_b(q):
        return remote(
            back.at[q], hin.at[rows(q), cols(q)], b_sem.at[0, q], b_sem.at[1, q], tm=base + q
        )

    @pl.loop(1, line)
    def _(o):
        out_b(other(o)).start()

    hin[rows(here), cols(here)] = back[here]
    for b in range(1, blocks):
        diagonal(b)

    @pl.loop(1, line)
    def _(o):
        in_b(other(o)).wait_recv()

    incoming = hin[...].astype(f32)
    for b in range(blocks):
        hb[b] = incoming.astype(bf16)
        incoming = incoming * totals[b] + states[b]

    share = steps // devices
    half = share // 2
    inner = channels * devices
    hit = iota((heads, channels), 0) == iota((heads, channels), 1) // hdim
    skip = jnp.sum(jnp.where(hit, column(d_skip[...]), 0.0), axis=0, keepdims=True)

    def product(k):
        at = aligned(k, share)
        yoff = jnp.dot(cc[at], hb[k * share // BLOCK], preferred_element_type=f32)
        y = yd[at] + yoff * ec[at] + skip * xa[at].astype(f32)
        gated = y * z[at]
        square = jnp.sum(gated * gated, axis=1, keepdims=True)
        sq[k] = jnp.broadcast_to(square, (share, share)).T[:1]
        scaled = (gated * norm_gain[...]).astype(bf16)
        part[at] = jnp.dot(scaled, w_out[...], preferred_element_type=f32).astype(bf16)

    def halves(k):
        begin = pl.multiple_of(k * share, share)
        return pl.ds(begin, half), pl.ds(pl.multiple_of(begin + half, half), half)

    top, bottom = pl.ds(0, half), pl.ds(half, half)
    right_top, right_bottom = halves(right)
    left_top, left_bottom = halves(left)
    across_top, across_bottom = halves(across)

    def go(n, src, dst, to):
        return remote(src, dst, send.at[n], recv.at[n], head=to)

    one = [
        go(0, part.at[across_top], first.at[0], right),
        go(1, part.at[across_bottom], first.at[1], left),
        go(2, part.at[right_bottom], full.at[0, bottom], right),
        go(3, part.at[left_top], full.at[1, top], left),
    ]

    def sq_copy(to, slot):
        return remote(sq.at[to], sqs.at[slot], sq_sem.at[0, to], sq_sem.at[1, slot], head=to)

    product(across)
    product(right)
    one[0].start()
    one[1].start()
    product(left)
    one[2].start()
    product(me)
    one[3].start()
    for to in (right, left, across):
        sq_copy(to, me).start()
    sqs[me] = sq[me]
    two = [
        go(4, stage.at[0], full.at[0, top], right),
        go(5, stage.at[1], full.at[1, bottom], left),
    ]
    for n, at in ((0, right_top), (1, left_bottom)):
        one[n].wait_recv()
        stage[n] = (part[at].astype(f32) + first[n].astype(f32)).astype(stage.dtype)
        two[n].start()
    for frm in (right, left, across):
        sq_copy(frm, frm).wait_recv()
    square = sqs[0]
    for k in range(1, devices):
        square = square + sqs[k]
    scale = lax.rsqrt(jnp.broadcast_to(square, (share, share)).T / inner + 1e-05)
    for copy in one[2:] + two:
        copy.wait_recv()
    own = aligned(me, share)
    own_rim = pl.ds(pl.multiple_of(me * share + RIM, RIM), share)
    for k in range(whole.shape[1] // share):
        at = pl.ds(k * share, share)
        total = part[own, at].astype(f32)
        total = total + full[0, :, at].astype(f32) + full[1, :, at].astype(f32)
        u = whole[own_rim, at].astype(f32) + emb[:, at]
        hid[own, at] = (u + scale * total).astype(hid.dtype)
    own_top, own_bottom = halves(me)
    three = [
        go(6, hid.at[own_top], hid.at[own_top], right),
        go(7, hid.at[own_bottom], hid.at[own_bottom], left),
        go(8, hid.at[own_bottom], hid.at[own_bottom], right),
        go(9, hid.at[own_top], hid.at[own_top], left),
    ]
    for copy in three:
        copy.start()
    four = [
        go(10, hid.at[left_top], hid.at[left_top], right),
        go(11, hid.at[right_bottom], hid.at[right_bottom], left),
    ]
    mix_cols = aligned(me, w_mix.shape[1])

    def finish(k):
        at = aligned(k, share)
        mixed = jnp.dot(hid[at], w_mix[...], preferred_element_type=f32)
        out[at] = (hid[at, mix_cols].astype(f32) + mixed).astype(out.dtype)

    for copy, following in zip(three[:2], four):
        copy.wait_recv()
        following.start()
    finish(me)
    for copy in three[2:]:
        copy.wait_recv()
    finish(left)
    finish(right)
    for copy in four:
        copy.wait_recv()
    finish(across)
    for copy in one + two + three + four:
        copy.wait_send()
    for to in (right, left, across):
        sq_copy(to, me).wait_send()
    for o in range(1, lines):
        for copy in line_copies(other_line(o), mine):
            copy.wait_send()

    @pl.loop(1, line)
    def _(o):
        q = other(o)
        out_g(q).wait_send()
        out_s(q).wait_send()
        out_b(q).wait_send()


def layer(tms, devices, whole, emb, in_gain, w_x, w_z, w_bc, w_dt, *rest):
    f32, bf16 = jnp.float32, jnp.bfloat16
    w_mix = rest[-1]
    rows, features = whole.shape
    steps, channels, state_n = rows - RIM, w_x.shape[1], w_bc.shape[1] // 2
    heads = w_dt.shape[0]
    blocks = steps // BLOCK
    share = steps // devices
    line = min(LINE, tms)
    lines = tms // line
    high, wide = 16, 128
    while (state_n // high) * (channels // wide) > line:
        if wide < channels:
            wide *= 2
        else:
            high *= 2
    scratch = [
        ((rows, features), bf16),
        ((rows, channels), f32),
        ((rows, 2 * state_n), f32),
        ((steps, channels), bf16),
        ((steps, state_n), bf16),
        ((steps, state_n), bf16),
        ((blocks, heads, BLOCK), f32),
        ((blocks, heads, BLOCK), f32),
        ((steps, 128), f32),
        ((steps, channels), f32),
        ((blocks, state_n, channels), f32),
        ((blocks, 1, channels), f32),
        ((state_n, channels), bf16),
        ((1, channels), f32),
        ((steps, channels), f32),
        ((steps, channels), f32),
        ((state_n, channels), bf16),
        ((blocks, state_n, channels), bf16),
        ((steps, features), bf16),
        ((devices, 1, share), f32),
        ((line, high, wide), bf16),
        ((line, 1, wide), f32),
        ((line, high, wide), f32),
        ((line, 1, wide), f32),
        ((line, high, wide), bf16),
        ((lines, high, wide), f32),
        ((lines, 1, wide), f32),
        ((steps, features), bf16),
        ((2, share // 2, features), bf16),
        ((2, share, features), bf16),
        ((2, share // 2, features), bf16),
        ((devices, 1, share), f32),
    ]
    args = (whole, emb, in_gain, w_x, w_z, w_bc, w_dt) + rest
    return pl.pallas_call(
        functools.partial(layer_kernel, tms, line, (high, wide), devices),
        out_shape=jax.ShapeDtypeStruct((steps, w_mix.shape[1]), bf16),
        in_specs=[VMEM] * len(args),
        out_specs=VMEM,
        scratch_shapes=[pltpu.VMEM(shape, kind) for shape, kind in scratch]
        + [
            DMA((2, line)),
            DMA((2, line)),
            DMA((2, lines)),
            DMA((2, lines)),
            DMA((2, line)),
            DMA((12,)),
            DMA((12,)),
            DMA((2, devices)),
        ],
        compiler_params=pltpu.CompilerParams(collective_id=1, has_side_effects=True),
        name="layer",
    )(*args)


def sinusoid(timestep, width):
    half = width // 2
    freq = jnp.exp(-math.log(10000.0) * jnp.arange(half, dtype=jnp.float32) / half)
    angle = timestep.astype(jnp.float32)[0] * freq
    return jnp.concatenate([jnp.sin(angle), jnp.cos(angle)])


def shards(
    latent,
    timestep,
    in_gain,
    w_x,
    w_z,
    w_bc,
    w_dt,
    conv_x,
    conv_bc,
    dt_bias,
    a_log,
    d_skip,
    norm_gain,
    w_out,
    w_mix,
):
    tms, devices = lax.axis_size("tm"), lax.axis_size("head")
    whole = gather(latent, tms, devices)
    return layer(
        tms,
        devices,
        whole,
        sinusoid(timestep, whole.shape[1])[None, :],
        in_gain[None, :],
        w_x,
        w_z,
        w_bc,
        w_dt.T,
        conv_x,
        conv_bc,
        dt_bias[None, :],
        a_log[None, :],
        d_skip[None, :],
        norm_gain[None, :],
        w_out,
        w_mix,
    )


def solution(mesh):
    in_specs = (
        P("tm", "head"),
        P(),
        P(),
        P(None, "head"),
        P(None, "head"),
        P(),
        P(None, "head"),
        P(None, "head"),
        P(),
        P("head"),
        P("head"),
        P("head"),
        P("head"),
        P("head", None),
        P(None, "head"),
    )
    out_specs = P("tm", "head")
    return jax.shard_map(shards, mesh=mesh, in_specs=in_specs, out_specs=out_specs, check_vma=False)
```

time: 141 us -> 88.7 us (0.63)
  matrix products: 21.5 us -> 0 us
  local copies, waits for them, and re-layouts: 21.2 us -> 1.67 us
  other arithmetic: 8.04 us -> 0.66 us
  Pallas kernels: 88.2 us -> 85.1 us
    dot_general x13 -> x0, matrix products: 21.5 us -> none  [the longest x2 4.47 us: shards(): yoff = jnp.dot(cmat, incoming.astype(bf16), preferred_element_type=f32)]
    reshape x7 -> x0, local copies, waits for them, and re-layouts: 10.2 us -> none  [the longest x4 7.14 us: spread(): return jnp.repeat(per_head, hdim, axis=-1)]
    slice x6 -> x0, local copies, waits for them, and re-layouts: 3.55 us -> none  [the longest x1 1.79 us: shards(): weighted = (xa[rows].astype(f32) * spread(tail, hdim)).astype(bf16)]
    broadcast_in_dim x11 -> x0, local copies, waits for them, and re-layouts: 3.05 us -> none  [spread(): return jnp.repeat(per_head, hdim, axis=-1)]
    pallas_call x2 -> x1, Pallas kernels: 70.2 us -> 67.3 us  [layer(): pl.pallas_call(functools.partial(layer_kernel, tms, line, (high, wide), d...]
    another operation x6 -> x0, other arithmetic: 1.96 us -> none
    reduce_sum x1 -> x0, other arithmetic: 1.69 us -> none  [shards(): jnp.mean(u * u, axis=1, keepdims=True) + 1e-05]
    exp x2 -> x0, local copies, waits for them, and re-layouts: 1.46 us -> none  [shards(): total = spread(jnp.exp(cum[-1:]), hdim)]
where the time goes in v2:
time: 88.7 us; the launch traced here: 88.1 us
  Pallas kernels  85.1 us (96%)
  local copies, waits for them, and re-layouts  1.67 us (2%)
    pallas_call x1, Pallas kernels, layer(): pl.pallas_call(functools.partial(layer_kernel, tms, line, (high, wide), d...  67.3 us
    pallas_call x1, Pallas kernels, gather(): pl.pallas_call(functools.partial(gather_kernel, tms, heads), out_shape=ja...  17.9 us

profile of v2, /device:TPU:1, one launch (start us, length us, event | category | flops | bytes accessed | tf_op | source)
XLA Modules:
  0.0 88.1 jit_solution(3576439300285930441)
XLA Ops:
  0.7 0.6 pad_maximum_fusion
  1.3 17.9 %gather_rows.1.whole = bf16[528,1024]{1,0:T(8,128)(2,1)} custom-call(bf16[512,256]{1,0:T(8,128)(2,1)} %lat.1), custom_call_target="tpu_custom_call" | custom-call | tf_op jit(solution)/shard_map/gather_rows/pallas_call | solution.py:104
  19.2 67.3 %layer.1 = bf16[512,256]{1,0:T(8,128)(2,1)} custom-call(bf16[528,1024]{1,0:T(8,128)(2,1)} %gather_rows.1.whole, f32[1,1024]{1,0:T(1,128)} %bitcast.9, f32[1,1024]{1,0:T(1,128)} %bitcast.10, bf16[1024,512]{1,0:T(8,128)(2,1)} %w_x.1, bf16[1024,512]{1,0:T(8,128)(2,1)} %w_z.1, bf16[1024,256]{1,0:T(8,128)(2,1)} %w_bc.1, bf16[8,1024]{1,0:T(8,128)(2,1)} %bitcast.8, ...), custom_call_target="tpu_custom_call" | custom-call | tf_op jit(solution)/shard_map/layer/pallas_call | solution.py:609
  86.5 1.7 %copy.18 = bf16[512,256]{1,0:T(8,128)(2,1)} copy(bf16[512,256]{1,0:T(8,128)(2,1)} %layer.1) | data formatting | bytes 524288
  (1 shorter events, 0.0 us)

commit v3 on v2

--- a/solution.py
+++ b/solution.py
@@ -13,6 +13,7 @@
 LINE = 32
 MESH = pl.DeviceIdType.MESH
 VMEM = pl.BlockSpec(memory_space=pltpu.VMEM)
+FAR = pl.BlockSpec(memory_space=pl.ANY)
 DMA = pltpu.SemaphoreType.DMA
 
 
@@ -149,9 +150,9 @@
     whole,
     emb,
     in_gain,
-    w_x,
-    w_z,
-    w_bc,
+    w_x_far,
+    w_z_far,
+    w_bc_far,
     w_dt,
     conv_x,
     conv_bc,
@@ -159,9 +160,14 @@
     a_log,
     d_skip,
     norm_gain,
+    w_out_far,
+    w_mix_far,
+    out,
+    w_x,
+    w_z,
+    w_bc,
     w_out,
     w_mix,
-    out,
     nrm,
     xs,
     bcs,
@@ -202,6 +208,7 @@
     send,
     recv,
     sq_sem,
+    w_sem,
 ):
     f32, bf16 = jnp.float32, jnp.bfloat16
     lines = tms // line
@@ -225,11 +232,19 @@
     def other_line(o):
         return lax.rem(mine + o, lines)
 
+    def far_first(i):
+        away = (i + 1) // 2
+        return other(line // 2 + jnp.where(lax.rem(i, 2) == 0, away, -away))
+
+    pairs = ((w_x_far, w_x), (w_bc_far, w_bc), (w_z_far, w_z), (w_out_far, w_out), (w_mix_far, w_mix))
+    loads = [pltpu.make_async_copy(far, near, w_sem.at[n]) for n, (far, near) in enumerate(pairs)]
+    for load in loads:
+        load.start()
     barrier = pltpu.get_barrier_semaphore()
 
-    @pl.loop(1, line)
-    def _(o):
-        pl.semaphore_signal(barrier, inc=1, device_id={"tm": base + other(o)}, device_id_type=MESH)
+    @pl.loop(0, line - 1)
+    def _(i):
+        pl.semaphore_signal(barrier, inc=1, device_id={"tm": base + far_first(i)}, device_id_type=MESH)
 
     for o in range(1, lines):
         pl.semaphore_signal(
@@ -252,7 +267,9 @@
     dt_t = lax.dot_general(
         w_dt[...], nrm[RIM:], (((1,), (1,)), ((), ())), preferred_element_type=f32
     )
+    loads[0].wait()
     xs[...] = jnp.dot(nrm[...], w_x[...], preferred_element_type=f32).astype(bf16).astype(f32)
+    loads[1].wait()
     bcs[...] = jnp.dot(nrm[...], w_bc[...], preferred_element_type=f32).astype(bf16).astype(f32)
 
     @pl.when(tm == 0)
@@ -331,9 +348,9 @@
     def in_g(q):
         return remote(g.at[:, cols(q)], gin.at[q], g_sem.at[0, q], g_sem.at[1, q], tm=base + q)
 
-    @pl.loop(1, line)
-    def _(o):
-        q = other(o)
+    @pl.loop(0, line - 1)
+    def _(i):
+        q = far_first(i)
         out_g(q).start()
         out_s(q).start()
 
@@ -392,6 +409,7 @@
     for o in range(1, lines):
         for copy in line_copies(other_line(o), mine):
             copy.start()
+    loads[2].wait()
     z[...] = jax.nn.silu(
         jnp.dot(nrm[RIM:], w_z[...], preferred_element_type=f32).astype(bf16).astype(f32)
     )
@@ -418,9 +436,9 @@
             back.at[q], hin.at[rows(q), cols(q)], b_sem.at[0, q], b_sem.at[1, q], tm=base + q
         )
 
-    @pl.loop(1, line)
-    def _(o):
-        out_b(other(o)).start()
+    @pl.loop(0, line - 1)
+    def _(i):
+        out_b(far_first(i)).start()
 
     hin[rows(here), cols(here)] = back[here]
     for b in range(1, blocks):
@@ -473,6 +491,7 @@
     def sq_copy(to, slot):
         return remote(sq.at[to], sqs.at[slot], sq_sem.at[0, to], sq_sem.at[1, slot], head=to)
 
+    loads[3].wait()
     product(across)
     product(right)
     one[0].start()
@@ -526,11 +545,12 @@
     def finish(k):
         at = aligned(k, share)
         mixed = jnp.dot(hid[at], w_mix[...], preferred_element_type=f32)
-        out[at] = (hid[at, mix_cols].astype(f32) + mixed).astype(out.dtype)
+        out[at] = hid[at, mix_cols].astype(f32) + mixed
 
     for copy, following in zip(three[:2], four):
         copy.wait_recv()
         following.start()
+    loads[4].wait()
     finish(me)
     for copy in three[2:]:
         copy.wait_recv()
@@ -571,7 +591,8 @@
             wide *= 2
         else:
             high *= 2
-    scratch = [
+    weights = (w_x, w_z, w_bc, rest[-2], w_mix)
+    scratch = [(w.shape, w.dtype) for w in weights] + [
         ((rows, features), bf16),
         ((rows, channels), f32),
         ((rows, 2 * state_n), f32),
@@ -608,8 +629,8 @@
     args = (whole, emb, in_gain, w_x, w_z, w_bc, w_dt) + rest
     return pl.pallas_call(
         functools.partial(layer_kernel, tms, line, (high, wide), devices),
-        out_shape=jax.ShapeDtypeStruct((steps, w_mix.shape[1]), bf16),
-        in_specs=[VMEM] * len(args),
+        out_shape=jax.ShapeDtypeStruct((steps, w_mix.shape[1]), f32),
+        in_specs=[FAR if any(a is w for w in weights) else VMEM for a in args],
         out_specs=VMEM,
         scratch_shapes=[pltpu.VMEM(shape, kind) for shape, kind in scratch]
         + [
@@ -621,6 +642,7 @@
             DMA((12,)),
             DMA((12,)),
             DMA((2, devices)),
+            DMA((len(weights),)),
         ],
         compiler_params=pltpu.CompilerParams(collective_id=1, has_side_effects=True),
         name="layer",
@@ -671,7 +693,7 @@
         norm_gain[None, :],
         w_out,
         w_mix,
-    )
+    ).astype(jnp.bfloat16)
 
 
 def solution(mesh):

time: 88.7 us -> 86.5 us (0.975); the launches traced: 88.1 us -> 85 us
  Pallas kernels: 85.1 us -> 81.9 us
  other arithmetic: 0.66 us -> 2.43 us
  local copies, waits for them, and re-layouts: 1.67 us -> 0 us
    pallas_call x1, Pallas kernels: 67.3 us -> 64 us  [layer(): pl.pallas_call(functools.partial(layer_kernel, tms, line, (high, wide), d...]
    convert_element_type x0 -> x1, other arithmetic: none -> 1.77 us  [shards(): return layer(tms, devices, whole, sinusoid(timestep, whole.shape[1])[None...]
    unnamed x1 -> x0, local copies, waits for them, and re-layouts: 1.67 us -> none
where the time goes in v3:
time: 86.5 us; the launch traced here: 85 us
  Pallas kernels  81.9 us (95%)
  other arithmetic  2.43 us (3%)
    pallas_call x1, Pallas kernels, layer(): pl.pallas_call(functools.partial(layer_kernel, tms, line, (high, wide), d...  64 us
    pallas_call x1, Pallas kernels, gather(): pl.pallas_call(functools.partial(gather_kernel, tms, heads), out_shape=ja...  17.9 us
    convert_element_type x1, other arithmetic, shards(): return layer(tms, devices, whole, sinusoid(timestep, whole.shape[1])[None...  1.77 us

profile of v3, /device:TPU:1, one launch (start us, length us, event | category | flops | bytes accessed | tf_op | source)
XLA Modules:
  0.0 85.0 jit_solution(17917107783095429683)
XLA Ops:
  0.7 0.6 pad_maximum_fusion
  1.3 17.9 %gather_rows.1.whole = bf16[528,1024]{1,0:T(8,128)(2,1)} custom-call(bf16[512,256]{1,0:T(8,128)(2,1)} %lat.1), custom_call_target="tpu_custom_call" | custom-call | tf_op jit(solution)/shard_map/gather_rows/pallas_call | solution.py:105
  19.2 64.0 %layer.1 = f32[512,256]{1,0:T(8,128)} custom-call(bf16[528,1024]{1,0:T(8,128)(2,1)} %gather_rows.1.whole, f32[1,1024]{1,0:T(1,128)} %bitcast.9, f32[1,1024]{1,0:T(1,128)} %bitcast.10, bf16[1024,512]{1,0:T(8,128)(2,1)} %w_x_far.1, bf16[1024,512]{1,0:T(8,128)(2,1)} %w_z_far.1, bf16[1024,256]{1,0:T(8,128)(2,1)} %w_bc_far.1, bf16[8,1024]{1,0:T(8,128)(2,1)} %bitcast.8, ...), custom_call_target="tpu_custom_call" | custom-call | tf_op jit(solution)/shard_map/layer/pallas_call | solution.py:630
  83.2 1.8 %convert_element_type.7 = bf16[512,256]{1,0:T(8,128)(2,1)} convert(f32[512,256]{1,0:T(8,128)} %layer.1) | non-fusion elementwise | flops 131072 | bytes 786432 | tf_op jit(solution)/shard_map/convert_element_type | solution.py:696
  (1 shorter events, 0.0 us)

commit v4 on v3

--- a/solution.py
+++ b/solution.py
@@ -469,98 +469,123 @@
         scaled = (gated * norm_gain[...]).astype(bf16)
         part[at] = jnp.dot(scaled, w_out[...], preferred_element_type=f32).astype(bf16)
 
-    def halves(k):
-        begin = pl.multiple_of(k * share, share)
-        return pl.ds(begin, half), pl.ds(pl.multiple_of(begin + half, half), half)
-
-    top, bottom = pl.ds(0, half), pl.ds(half, half)
-    right_top, right_bottom = halves(right)
-    left_top, left_bottom = halves(left)
-    across_top, across_bottom = halves(across)
+    features = whole.shape[1]
+    low, up = pl.ds(0, features // 2), pl.ds(features // 2, features // 2)
+
+    def half_of(k, n):
+        return pl.ds(pl.multiple_of(k * share + n * half, half), half)
 
     def go(n, src, dst, to):
         return remote(src, dst, send.at[n], recv.at[n], head=to)
 
-    one = [
-        go(0, part.at[across_top], first.at[0], right),
-        go(1, part.at[across_bottom], first.at[1], left),
-        go(2, part.at[right_bottom], full.at[0, bottom], right),
-        go(3, part.at[left_top], full.at[1, top], left),
-    ]
+    def sums(n):
+        at = pl.ds(n * half, half)
+        base_sem = 12 * n
+        return (
+            [
+                go(base_sem, part.at[half_of(across, n), low], first.at[0, at], right),
+                go(base_sem + 1, part.at[half_of(across, n), up], first.at[1, at], left),
+                go(base_sem + 2, part.at[half_of(right, n), up], full.at[0, at, up], right),
+                go(base_sem + 3, part.at[half_of(left, n), low], full.at[1, at, low], left),
+            ],
+            [
+                go(base_sem + 4, stage.at[0, at], full.at[0, at, low], right),
+                go(base_sem + 5, stage.at[1, at], full.at[1, at, up], left),
+            ],
+        )
+
+    def hides(n):
+        own, lefts, rights = half_of(me, n), half_of(left, n), half_of(right, n)
+        base_sem = 12 * n
+        return (
+            [
+                go(base_sem + 6, hid.at[own, low], hid.at[own, low], right),
+                go(base_sem + 7, hid.at[own, up], hid.at[own, up], left),
+                go(base_sem + 8, hid.at[own, up], hid.at[own, up], right),
+                go(base_sem + 9, hid.at[own, low], hid.at[own, low], left),
+            ],
+            [
+                go(base_sem + 10, hid.at[lefts, low], hid.at[lefts, low], right),
+                go(base_sem + 11, hid.at[rights, up], hid.at[rights, up], left),
+            ],
+        )
 
     def sq_copy(to, slot):
         return remote(sq.at[to], sqs.at[slot], sq_sem.at[0, to], sq_sem.at[1, slot], head=to)
 
+    ones, twos = zip(*[sums(n) for n in range(2)])
+    threes, fours = zip(*[hides(n) for n in range(2)])
     loads[3].wait()
     product(across)
     product(right)
-    one[0].start()
-    one[1].start()
+    ones[0][0].start()
+    ones[0][1].start()
     product(left)
-    one[2].start()
+    ones[0][2].start()
+    ones[0][3].start()
     product(me)
-    one[3].start()
     for to in (right, left, across):
         sq_copy(to, me).start()
+    for copy in ones[1][:2]:
+        copy.start()
     sqs[me] = sq[me]
-    two = [
-        go(4, stage.at[0], full.at[0, top], right),
-        go(5, stage.at[1], full.at[1, bottom], left),
-    ]
-    for n, at in ((0, right_top), (1, left_bottom)):
-        one[n].wait_recv()
-        stage[n] = (part[at].astype(f32) + first[n].astype(f32)).astype(stage.dtype)
-        two[n].start()
+
+    def pass_on(n):
+        at = pl.ds(n * half, half)
+        for d, k, lanes in ((0, right, low), (1, left, up)):
+            ones[n][d].wait_recv()
+            value = part[half_of(k, n), lanes].astype(f32) + first[d, at].astype(f32)
+            stage[d, at] = value.astype(stage.dtype)
+            twos[n][d].start()
+
+    pass_on(0)
+    for copy in ones[1][2:]:
+        copy.start()
+    pass_on(1)
     for frm in (right, left, across):
         sq_copy(frm, frm).wait_recv()
     square = sqs[0]
     for k in range(1, devices):
         square = square + sqs[k]
     scale = lax.rsqrt(jnp.broadcast_to(square, (share, share)).T / inner + 1e-05)
-    for copy in one[2:] + two:
-        copy.wait_recv()
-    own = aligned(me, share)
-    own_rim = pl.ds(pl.multiple_of(me * share + RIM, RIM), share)
-    for k in range(whole.shape[1] // share):
-        at = pl.ds(k * share, share)
-        total = part[own, at].astype(f32)
-        total = total + full[0, :, at].astype(f32) + full[1, :, at].astype(f32)
-        u = whole[own_rim, at].astype(f32) + emb[:, at]
-        hid[own, at] = (u + scale * total).astype(hid.dtype)
-    own_top, own_bottom = halves(me)
-    three = [
-        go(6, hid.at[own_top], hid.at[own_top], right),
-        go(7, hid.at[own_bottom], hid.at[own_bottom], left),
-        go(8, hid.at[own_bottom], hid.at[own_bottom], right),
-        go(9, hid.at[own_top], hid.at[own_top], left),
-    ]
-    for copy in three:
-        copy.start()
-    four = [
-        go(10, hid.at[left_top], hid.at[left_top], right),
-        go(11, hid.at[right_bottom], hid.at[right_bottom], left),
-    ]
+    for n in range(2):
+        for copy in ones[n][2:] + twos[n]:
+            copy.wait_recv()
+        at, own = pl.ds(n * half, half), half_of(me, n)
+        own_rim = pl.ds(pl.multiple_of(me * share + n * half + RIM, RIM), half)
+        for k in range(features // share):
+            lanes = pl.ds(k * share, share)
+            total = part[own, lanes].astype(f32)
+            total = total + full[0, at, lanes].astype(f32) + full[1, at, lanes].astype(f32)
+            u = whole[own_rim, lanes].astype(f32) + emb[:, lanes]
+            hid[own, lanes] = (u + scale[n * half : (n + 1) * half] * total).astype(hid.dtype)
+        for copy in threes[n]:
+            copy.start()
     mix_cols = aligned(me, w_mix.shape[1])
 
-    def finish(k):
-        at = aligned(k, share)
+    def finish(at):
         mixed = jnp.dot(hid[at], w_mix[...], preferred_element_type=f32)
         out[at] = hid[at, mix_cols].astype(f32) + mixed
 
-    for copy, following in zip(three[:2], four):
-        copy.wait_recv()
-        following.start()
-    loads[4].wait()
-    finish(me)
-    for copy in three[2:]:
-        copy.wait_recv()
-    finish(left)
-    finish(right)
-    for copy in four:
-        copy.wait_recv()
-    finish(across)
-    for copy in one + two + three + four:
-        copy.wait_send()
+    for n in range(2):
+        for copy, following in zip(threes[n][:2], fours[n]):
+            copy.wait_recv()
+            following.start()
+        if n == 0:
+            loads[4].wait()
+            finish(aligned(me, share))
+    for n in range(2):
+        for copy in threes[n][2:]:
+            copy.wait_recv()
+    finish(aligned(left, share))
+    finish(aligned(right, share))
+    for n in range(2):
+        for copy in fours[n]:
+            copy.wait_recv()
+        finish(half_of(across, n))
+    for n in range(2):
+        for copy in ones[n] + twos[n] + threes[n] + fours[n]:
+            copy.wait_send()
     for to in (right, left, across):
         sq_copy(to, me).wait_send()
     for o in range(1, lines):
@@ -621,9 +646,9 @@
         ((lines, high, wide), f32),
         ((lines, 1, wide), f32),
         ((steps, features), bf16),
-        ((2, share // 2, features), bf16),
+        ((2, share, features // 2), bf16),
         ((2, share, features), bf16),
-        ((2, share // 2, features), bf16),
+        ((2, share, features // 2), bf16),
         ((devices, 1, share), f32),
     ]
     args = (whole, emb, in_gain, w_x, w_z, w_bc, w_dt) + rest
@@ -639,8 +664,8 @@
             DMA((2, lines)),
             DMA((2, lines)),
             DMA((2, line)),
-            DMA((12,)),
-            DMA((12,)),
+            DMA((24,)),
+            DMA((24,)),
             DMA((2, devices)),
             DMA((len(weights),)),
         ],

time: 86.5 us -> 85.6 us (0.990); the launches traced: 85 us -> 85.2 us
  no operation moved by 1% of the time
where the time goes in v4:
time: 85.6 us; the launch traced here: 85.2 us
  Pallas kernels  82.1 us (96%)
  other arithmetic  2.43 us (3%)
    pallas_call x1, Pallas kernels, layer(): pl.pallas_call(functools.partial(layer_kernel, tms, line, (high, wide), d...  64.2 us
    pallas_call x1, Pallas kernels, gather(): pl.pallas_call(functools.partial(gather_kernel, tms, heads), out_shape=ja...  17.9 us
    convert_element_type x1, other arithmetic, shards(): return layer(tms, devices, whole, sinusoid(timestep, whole.shape[1])[None...  1.77 us

profile of v4, /device:TPU:1, one launch (start us, length us, event | category | flops | bytes accessed | tf_op | source)
XLA Modules:
  0.0 85.2 jit_solution(11388070367155221078)
XLA Ops:
  0.7 0.6 pad_maximum_fusion
  1.3 17.9 %gather_rows.1.whole = bf16[528,1024]{1,0:T(8,128)(2,1)} custom-call(bf16[512,256]{1,0:T(8,128)(2,1)} %lat.1), custom_call_target="tpu_custom_call" | custom-call | tf_op jit(solution)/shard_map/gather_rows/pallas_call | solution.py:105
  19.2 64.2 %layer.1 = f32[512,256]{1,0:T(8,128)} custom-call(bf16[528,1024]{1,0:T(8,128)(2,1)} %gather_rows.1.whole, f32[1,1024]{1,0:T(1,128)} %bitcast.9, f32[1,1024]{1,0:T(1,128)} %bitcast.10, bf16[1024,512]{1,0:T(8,128)(2,1)} %w_x_far.1, bf16[1024,512]{1,0:T(8,128)(2,1)} %w_z_far.1, bf16[1024,256]{1,0:T(8,128)(2,1)} %w_bc_far.1, bf16[8,1024]{1,0:T(8,128)(2,1)} %bitcast.8, ...), custom_call_target="tpu_custom_call" | custom-call | tf_op jit(solution)/shard_map/layer/pallas_call | solution.py:655
  83.4 1.8 %convert_element_type.7 = bf16[512,256]{1,0:T(8,128)(2,1)} convert(f32[512,256]{1,0:T(8,128)} %layer.1) | non-fusion elementwise | flops 131072 | bytes 786432 | tf_op jit(solution)/shard_map/convert_element_type | solution.py:721
  (1 shorter events, 0.0 us)

commit v5 on v4

--- a/solution.py
+++ b/solution.py
@@ -200,6 +200,15 @@
     full,
     stage,
     sqs,
+    pg,
+    ps,
+    sf,
+    gf,
+    gc,
+    sc,
+    hc,
+    give,
+    got,
     s_sem,
     g_sem,
     xt_sem,
@@ -209,12 +218,16 @@
     recv,
     sq_sem,
     w_sem,
+    pair_sem,
 ):
     f32, bf16 = jnp.float32, jnp.bfloat16
     lines = tms // line
     tm = lax.axis_index("tm")
-    here, mine = lax.rem(tm, line), tm // line
-    base = mine * line
+    chips = line // 2
+    place, mine = lax.rem(tm, line), tm // line
+    here, core = place // 2, lax.rem(place, 2)
+    base = mine * line + core
+    partner = tm + 1 - 2 * core
     high, wide = piece
     stack = s.shape[0] // high
     me = lax.axis_index("head")
@@ -227,14 +240,14 @@
         return aligned(k // stack, wide)
 
     def other(o):
-        return lax.rem(here + o, line)
+        return lax.rem(here + o, chips)
 
     def other_line(o):
         return lax.rem(mine + o, lines)
 
     def far_first(i):
         away = (i + 1) // 2
-        return other(line // 2 + jnp.where(lax.rem(i, 2) == 0, away, -away))
+        return other(chips // 2 + jnp.where(lax.rem(i, 2) == 0, away, -away))
 
     pairs = ((w_x_far, w_x), (w_bc_far, w_bc), (w_z_far, w_z), (w_out_far, w_out), (w_mix_far, w_mix))
     loads = [pltpu.make_async_copy(far, near, w_sem.at[n]) for n, (far, near) in enumerate(pairs)]
@@ -242,14 +255,15 @@
         load.start()
     barrier = pltpu.get_barrier_semaphore()
 
-    @pl.loop(0, line - 1)
+    @pl.loop(0, chips - 1)
     def _(i):
-        pl.semaphore_signal(barrier, inc=1, device_id={"tm": base + far_first(i)}, device_id_type=MESH)
+        pl.semaphore_signal(barrier, inc=1, device_id={"tm": base + 2 * far_first(i)}, device_id_type=MESH)
 
     for o in range(1, lines):
         pl.semaphore_signal(
-            barrier, inc=1, device_id={"tm": other_line(o) * line + here}, device_id_type=MESH
-        )
+            barrier, inc=1, device_id={"tm": other_line(o) * line + place}, device_id_type=MESH
+        )
+    pl.semaphore_signal(barrier, inc=1, device_id={"tm": partner}, device_id_type=MESH)
     for device in (left, right, across):
         pl.semaphore_signal(barrier, inc=1, device_id={"head": device}, device_id_type=MESH)
 
@@ -334,28 +348,49 @@
         run_state, run_total = run_state * totals[b] + states[b], run_total * totals[b]
     s[...] = run_state.astype(bf16)
     g[...] = run_total
-    pl.semaphore_wait(barrier, line - 1 + lines - 1 + 3)
+    pl.semaphore_wait(barrier, chips - 1 + 1 + lines - 1 + 3)
+
+    keep, cede = aligned(core, channels // 2), aligned(1 - core, channels // 2)
+
+    def pair(n, src, dst):
+        return remote(src, dst, pair_sem.at[0, n], pair_sem.at[1, n], tm=partner)
+
+    pairs_out = [pair(0, g.at[:, cede], pg), pair(1, s.at[:, cede], ps)]
+    for copy in pairs_out:
+        copy.start()
+    for copy in pairs_out:
+        copy.wait_recv()
+
+    def ordered(own, others):
+        return jnp.where(core == 0, own, others), jnp.where(core == 0, others, own)
+
+    first_s, second_s = ordered(s[:, keep].astype(f32), ps[...].astype(f32))
+    first_g, second_g = ordered(g[:, keep], pg[...])
+    sf[...] = first_s
+    gf[...] = first_g
+    gc[...] = first_g * second_g
+    sc[...] = (first_s * second_g + second_s).astype(bf16)
 
     def out_s(q):
-        return remote(s.at[rows(q), cols(q)], sin.at[here], s_sem.at[0, q], s_sem.at[1, here], tm=base + q)
+        return remote(sc.at[rows(q), cols(q)], sin.at[here], s_sem.at[0, q], s_sem.at[1, here], tm=base + 2 * q)
 
     def out_g(q):
-        return remote(g.at[:, cols(q)], gin.at[here], g_sem.at[0, q], g_sem.at[1, here], tm=base + q)
+        return remote(gc.at[:, cols(q)], gin.at[here], g_sem.at[0, q], g_sem.at[1, here], tm=base + 2 * q)
 
     def in_s(q):
-        return remote(s.at[rows(q), cols(q)], sin.at[q], s_sem.at[0, q], s_sem.at[1, q], tm=base + q)
+        return remote(sc.at[rows(q), cols(q)], sin.at[q], s_sem.at[0, q], s_sem.at[1, q], tm=base + 2 * q)
 
     def in_g(q):
-        return remote(g.at[:, cols(q)], gin.at[q], g_sem.at[0, q], g_sem.at[1, q], tm=base + q)
-
-    @pl.loop(0, line - 1)
+        return remote(gc.at[:, cols(q)], gin.at[q], g_sem.at[0, q], g_sem.at[1, q], tm=base + 2 * q)
+
+    @pl.loop(0, chips - 1)
     def _(i):
         q = far_first(i)
         out_g(q).start()
         out_s(q).start()
 
-    sin[here] = s[rows(here), cols(here)]
-    gin[here] = g[:, cols(here)]
+    sin[here] = sc[rows(here), cols(here)]
+    gin[here] = gc[:, cols(here)]
 
     def diagonal(b):
         at = aligned(b, BLOCK)
@@ -394,13 +429,13 @@
         return state * factor + sin[k].astype(f32), decay * factor
 
     state, decay = lax.fori_loop(
-        0, line, step, (jnp.zeros((high, wide), f32), jnp.ones((1, wide), f32))
+        0, chips, step, (jnp.zeros((high, wide), f32), jnp.ones((1, wide), f32))
     )
     xt[mine] = state
     xd[mine] = decay
 
     def line_copies(q, slot):
-        device = q * line + here
+        device = q * line + place
         return (
             remote(xt.at[slot], xt.at[slot], xt_sem.at[0, q], xt_sem.at[1, slot], tm=device),
             remote(xd.at[slot], xd.at[slot], xd_sem.at[0, q], xd_sem.at[1, slot], tm=device),
@@ -424,31 +459,39 @@
         back[k] = (start * dec[k] + pre[k]).astype(back.dtype)
         return carry
 
-    lax.fori_loop(0, line, final, 0)
+    lax.fori_loop(0, chips, final, 0)
 
     def out_b(q):
         return remote(
-            back.at[q], hin.at[rows(here), cols(here)], b_sem.at[0, q], b_sem.at[1, here], tm=base + q
+            back.at[q], hc.at[rows(here), cols(here)], b_sem.at[0, q], b_sem.at[1, here], tm=base + 2 * q
         )
 
     def in_b(q):
         return remote(
-            back.at[q], hin.at[rows(q), cols(q)], b_sem.at[0, q], b_sem.at[1, q], tm=base + q
-        )
-
-    @pl.loop(0, line - 1)
+            back.at[q], hc.at[rows(q), cols(q)], b_sem.at[0, q], b_sem.at[1, q], tm=base + 2 * q
+        )
+
+    @pl.loop(0, chips - 1)
     def _(i):
         out_b(far_first(i)).start()
 
-    hin[rows(here), cols(here)] = back[here]
+    hc[rows(here), cols(here)] = back[here]
     for b in range(1, blocks):
         diagonal(b)
 
-    @pl.loop(1, line)
+    @pl.loop(1, chips)
     def _(o):
         in_b(other(o)).wait_recv()
 
-    incoming = hin[...].astype(f32)
+    before = hc[...].astype(f32)
+    own, others = ordered(before, before * gf[...] + sf[...])
+    give[...] = others.astype(bf16)
+    pair_back = pair(2, give, got)
+    pair_back.start()
+    hin[:, keep] = own
+    pair_back.wait_recv()
+    hin[:, cede] = got[...].astype(f32)
+    incoming = hin[...]
     for b in range(blocks):
         hb[b] = incoming.astype(bf16)
         incoming = incoming * totals[b] + states[b]
@@ -588,11 +631,13 @@
             copy.wait_send()
     for to in (right, left, across):
         sq_copy(to, me).wait_send()
+    for copy in pairs_out + [pair_back]:
+        copy.wait_send()
     for o in range(1, lines):
         for copy in line_copies(other_line(o), mine):
             copy.wait_send()
 
-    @pl.loop(1, line)
+    @pl.loop(1, chips)
     def _(o):
         q = other(o)
         out_g(q).wait_send()
@@ -611,8 +656,9 @@
     line = min(LINE, tms)
     lines = tms // line
     high, wide = 16, 128
-    while (state_n // high) * (channels // wide) > line:
-        if wide < channels:
+    chips, kept = line // 2, channels // 2
+    while (state_n // high) * (kept // wide) > chips:
+        if wide < kept:
             wide *= 2
         else:
             high *= 2
@@ -634,15 +680,15 @@
         ((1, channels), f32),
         ((steps, channels), f32),
         ((steps, channels), f32),
-        ((state_n, channels), bf16),
+        ((state_n, channels), f32),
         ((blocks, state_n, channels), bf16),
         ((steps, features), bf16),
         ((devices, 1, share), f32),
-        ((line, high, wide), bf16),
-        ((line, 1, wide), f32),
-        ((line, high, wide), f32),
-        ((line, 1, wide), f32),
-        ((line, high, wide), bf16),
+        ((chips, high, wide), bf16),
+        ((chips, 1, wide), f32),
+        ((chips, high, wide), f32),
+        ((chips, 1, wide), f32),
+        ((chips, high, wide), bf16),
         ((lines, high, wide), f32),
         ((lines, 1, wide), f32),
         ((steps, features), bf16),
@@ -650,6 +696,15 @@
         ((2, share, features), bf16),
         ((2, share, features // 2), bf16),
         ((devices, 1, share), f32),
+        ((1, kept), f32),
+        ((state_n, kept), bf16),
+        ((state_n, kept), f32),
+        ((1, kept), f32),
+        ((1, kept), f32),
+        ((state_n, kept), bf16),
+        ((state_n, kept), bf16),
+        ((state_n, kept), bf16),
+        ((state_n, kept), bf16),
     ]
     args = (whole, emb, in_gain, w_x, w_z, w_bc, w_dt) + rest
     return pl.pallas_call(
@@ -659,15 +714,16 @@
         out_specs=VMEM,
         scratch_shapes=[pltpu.VMEM(shape, kind) for shape, kind in scratch]
         + [
-            DMA((2, line)),
-            DMA((2, line)),
+            DMA((2, chips)),
+            DMA((2, chips)),
             DMA((2, lines)),
             DMA((2, lines)),
-            DMA((2, line)),
+            DMA((2, chips)),
             DMA((24,)),
             DMA((24,)),
             DMA((2, devices)),
             DMA((len(weights),)),
+            DMA((2, 3)),
         ],
         compiler_params=pltpu.CompilerParams(collective_id=1, has_side_effects=True),
         name="layer",

time: 85.6 us -> 82.8 us (0.967)
  Pallas kernels: 82.1 us -> 79.5 us
    pallas_call x1, Pallas kernels: 64.2 us -> 61.6 us  [layer(): pl.pallas_call(functools.partial(layer_kernel, tms, line, (high, wide), d...]
where the time goes in v5:
time: 82.8 us; the launch traced here: 82.6 us
  Pallas kernels  79.5 us (96%)
  other arithmetic  2.43 us (3%)
    pallas_call x1, Pallas kernels, layer(): pl.pallas_call(functools.partial(layer_kernel, tms, line, (high, wide), d...  61.6 us
    pallas_call x1, Pallas kernels, gather(): pl.pallas_call(functools.partial(gather_kernel, tms, heads), out_shape=ja...  17.9 us
    convert_element_type x1, other arithmetic, shards(): return layer(tms, devices, whole, sinusoid(timestep, whole.shape[1])[None...  1.77 us

profile of v5, /device:TPU:1, one launch (start us, length us, event | category | flops | bytes accessed | tf_op | source)
XLA Modules:
  0.0 82.6 jit_solution(3366225783857770764)
XLA Ops:
  0.7 0.6 pad_maximum_fusion
  1.3 17.9 %gather_rows.1.whole = bf16[528,1024]{1,0:T(8,128)(2,1)} custom-call(bf16[512,256]{1,0:T(8,128)(2,1)} %lat.1), custom_call_target="tpu_custom_call" | custom-call | tf_op jit(solution)/shard_map/gather_rows/pallas_call | solution.py:105
  19.2 61.6 %layer.1 = f32[512,256]{1,0:T(8,128)} custom-call(bf16[528,1024]{1,0:T(8,128)(2,1)} %gather_rows.1.whole, f32[1,1024]{1,0:T(1,128)} %bitcast.9, f32[1,1024]{1,0:T(1,128)} %bitcast.10, bf16[1024,512]{1,0:T(8,128)(2,1)} %w_x_far.1, bf16[1024,512]{1,0:T(8,128)(2,1)} %w_z_far.1, bf16[1024,256]{1,0:T(8,128)(2,1)} %w_bc_far.1, bf16[8,1024]{1,0:T(8,128)(2,1)} %bitcast.8, ...), custom_call_target="tpu_custom_call" | custom-call | tf_op jit(solution)/shard_map/layer/pallas_call | solution.py:710
  80.8 1.8 %convert_element_type.7 = bf16[512,256]{1,0:T(8,128)(2,1)} convert(f32[512,256]{1,0:T(8,128)} %layer.1) | non-fusion elementwise | flops 131072 | bytes 786432 | tf_op jit(solution)/shard_map/convert_element_type | solution.py:777
  (1 shorter events, 0.0 us)

commit v6 on v5

--- a/solution.py
+++ b/solution.py
@@ -108,7 +108,10 @@
         in_specs=[VMEM],
         out_specs=VMEM,
         scratch_shapes=[DMA, DMA((6,)), DMA((6,)), DMA((heads,)), DMA((heads,))],
-        compiler_params=pltpu.CompilerParams(collective_id=0, has_side_effects=True),
+        compiler_params=pltpu.CompilerParams(
+            collective_id=0, has_side_effects=True, vmem_limit_bytes=8 * 2**20
+        ),
+        cost_estimate=pl.CostEstimate(flops=10**10, bytes_accessed=30 * 2**20, transcendentals=0),
         name="gather_rows",
     )(lat)
 
@@ -725,7 +728,9 @@
             DMA((len(weights),)),
             DMA((2, 3)),
         ],
-        compiler_params=pltpu.CompilerParams(collective_id=1, has_side_effects=True),
+        compiler_params=pltpu.CompilerParams(
+            collective_id=1, has_side_effects=True, vmem_limit_bytes=32 * 2**20
+        ),
         name="layer",
     )(*args)
 

time: 82.8 us -> 78.7 us (0.950)
  Pallas kernels: 79.5 us -> 75.9 us
  other arithmetic: 2.43 us -> 0.79 us
  local copies, waits for them, and re-layouts: 0 us -> 1.02 us
    pallas_call x1, Pallas kernels: 61.6 us -> 59.7 us  [layer(): pl.pallas_call(functools.partial(layer_kernel, tms, line, (high, wide), d...]
    pallas_call x1, Pallas kernels: 17.9 us -> 16.1 us  [gather(): pl.pallas_call(functools.partial(gather_kernel, tms, heads), out_shape=ja...]
    convert_element_type x1, other arithmetic: 1.77 us -> 0.73 us  [shards(): return layer(tms, devices, whole, sinusoid(timestep, whole.shape[1])[None...]
    unnamed x0 -> x28, local copies, waits for them, and re-layouts: none -> 1.02 us
where the time goes in v6:
time: 78.7 us; the launch traced here: 78.5 us
  Pallas kernels  75.9 us (96%)
  local copies, waits for them, and re-layouts  1.02 us (1%)
  between operations  0.87 us (1%)
  other arithmetic  0.79 us (1%)
    pallas_call x1, Pallas kernels, layer(): pl.pallas_call(functools.partial(layer_kernel, tms, line, (high, wide), d...  59.7 us
    pallas_call x1, Pallas kernels, gather(): pl.pallas_call(functools.partial(gather_kernel, tms, heads), out_shape=ja...  16.1 us

profile of v6, /device:TPU:1, one launch (start us, length us, event | category | flops | bytes accessed | tf_op | source)
XLA Modules:
  0.0 78.5 jit_solution(11342654388874464312)
XLA Ops:
  0.7 0.0 copy-start.13
  0.7 0.9 %copy-done.13 = bf16[512,256]{1,0:T(8,128)(2,1)S(1)} copy-done((bf16[512,256]{1,0:T(8,128)(2,1)S(1)}, bf16[512,256]{1,0:T(8,128)(2,1)}, u32[]{:S(2)}) %copy-start.13) | copy-done | bytes 262168
  1.7 0.0 copy-start
  1.7 0.0 copy-start.1
  1.7 0.0 copy-start.2
  1.7 0.0 copy-start.3
  1.7 0.0 copy-start.4
  1.7 0.0 copy-start.5
  1.7 0.0 copy-start.6
  1.7 0.0 copy-start.7
  1.7 0.0 copy-start.8
  1.7 0.0 copy-start.9
  1.8 0.0 copy-start.10
  1.8 0.0 copy-start.11
  1.8 0.0 copy-start.12
  1.8 16.1 %gather_rows.1.whole = bf16[528,1024]{1,0:T(8,128)(2,1)S(1)} custom-call(bf16[512,256]{1,0:T(8,128)(2,1)S(1)} %copy-done.13), custom_call_target="tpu_custom_call" | custom-call | flops 10000000000 | bytes 31457280 | tf_op jit(solution)/shard_map/gather_rows/pallas_call | solution.py:105
  17.9 0.0 copy-done
  17.9 0.0 copy-done.1
  17.9 0.0 copy-done.2
  17.9 0.0 copy-done.3
  17.9 0.0 copy-done.4
  18.0 0.0 copy-done.5
  18.0 0.0 copy-done.6
  18.0 0.0 copy-done.7
  18.0 0.0 copy-done.8
  18.0 0.0 copy-done.9
  18.0 0.0 copy-done.10
  18.0 0.0 copy-done.11
  18.0 0.0 copy-done.12
  18.0 59.7 %layer.1 = f32[512,256]{1,0:T(8,128)S(1)} custom-call(bf16[528,1024]{1,0:T(8,128)(2,1)S(1)} %gather_rows.1.whole, f32[1,1024]{1,0:T(1,128)S(1)} %bitcast.9, f32[1,1024]{1,0:T(1,128)S(1)} %bitcast.10, bf16[1024,512]{1,0:T(8,128)(2,1)S(1)} %copy-done, bf16[1024,512]{1,0:T(8,128)(2,1)S(1)} %copy-done.1, bf16[1024,256]{1,0:T(8,128)(2,1)S(1)} %copy-done.3, ...), custom_call_target="tpu_custom_call" | custom-call | tf_op jit(solution)/shard_map/layer/pallas_call | solution.py:713
  77.8 0.7 convert_element_type.7
  (2 shorter events, 0.1 us)
Async XLA Ops:
  0.7 1.0 %copy-start.13 = (bf16[512,256]{1,0:T(8,128)(2,1)S(1)}, bf16[512,256]{1,0:T(8,128)(2,1)}, u32[]{:S(2)}) copy-start(bf16[512,256]{1,0:T(8,128)(2,1)} %lat.1) | copy-start | bytes 786436
  1.7 16.2 %copy-start = (bf16[1024,512]{1,0:T(8,128)(2,1)S(1)}, bf16[1024,512]{1,0:T(8,128)(2,1)}, u32[]{:S(2)}) copy-start(bf16[1024,512]{1,0:T(8,128)(2,1)} %w_x_far.1) | copy-start | bytes 3145732
  1.7 16.2 %copy-start.1 = (bf16[1024,512]{1,0:T(8,128)(2,1)S(1)}, bf16[1024,512]{1,0:T(8,128)(2,1)}, u32[]{:S(2)}) copy-start(bf16[1024,512]{1,0:T(8,128)(2,1)} %w_z_far.1) | copy-start | bytes 3145732
  1.7 16.3 %copy-start.2 = (bf16[512,1024]{1,0:T(8,128)(2,1)S(1)}, bf16[512,1024]{1,0:T(8,128)(2,1)}, u32[]{:S(2)}) copy-start(bf16[512,1024]{1,0:T(8,128)(2,1)} %w_out_far.1) | copy-start | bytes 3145732
  1.7 16.3 %copy-start.3 = (bf16[1024,256]{1,0:T(8,128)(2,1)S(1)}, bf16[1024,256]{1,0:T(8,128)(2,1)}, u32[]{:S(2)}) copy-start(bf16[1024,256]{1,0:T(8,128)(2,1)} %w_bc_far.1) | copy-start | bytes 1572868
  1.7 16.3 %copy-start.4 = (bf16[1024,256]{1,0:T(8,128)(2,1)S(1)}, bf16[1024,256]{1,0:T(8,128)(2,1)}, u32[]{:S(2)}) copy-start(bf16[1024,256]{1,0:T(8,128)(2,1)} %w_mix_far.1) | copy-start | bytes 1572868
  1.7 16.3 %copy-start.5 = (bf16[1024,8]{0,1:T(8,128)(2,1)S(1)}, bf16[1024,8]{0,1:T(8,128)(2,1)}, u32[]{:S(2)}) copy-start(bf16[1024,8]{0,1:T(8,128)(2,1)} %param.21) | copy-start | bytes 49156
  1.7 16.3 %copy-start.6 = (f32[4,512]{1,0:T(4,128)S(1)}, f32[4,512]{1,0:T(4,128)}, u32[]{:S(2)}) copy-start(f32[4,512]{1,0:T(4,128)} %conv_x.1) | copy-start | bytes 24580
  1.7 16.3 %copy-start.7 = (f32[1024]{0:T(1024)S(1)}, f32[1024]{0:T(1024)}, u32[]{:S(2)}) copy-start(f32[1024]{0:T(1024)} %param.17) | copy-start | bytes 12292
  1.7 16.3 %copy-start.8 = (f32[4,256]{1,0:T(4,128)S(1)}, f32[4,256]{1,0:T(4,128)}, u32[]{:S(2)}) copy-start(f32[4,256]{1,0:T(4,128)} %conv_bc.1) | copy-start | bytes 12292
  1.7 16.3 %copy-start.9 = (f32[512]{0:T(512)S(1)}, f32[512]{0:T(512)}, u32[]{:S(2)}) copy-start(f32[512]{0:T(512)} %param.27) | copy-start | bytes 6148
  1.8 16.3 %copy-start.10 = (f32[8]{0:T(128)S(1)}, f32[8]{0:T(128)}, u32[]{:S(2)}) copy-start(f32[8]{0:T(128)} %param.24) | copy-start | bytes 100
  1.8 16.3 %copy-start.11 = (f32[8]{0:T(128)S(1)}, f32[8]{0:T(128)}, u32[]{:S(2)}) copy-start(f32[8]{0:T(128)} %param.25) | copy-start | bytes 100
  1.8 16.2 %copy-start.12 = (f32[8]{0:T(128)S(1)}, f32[8]{0:T(128)}, u32[]{:S(2)}) copy-start(f32[8]{0:T(128)} %param.26) | copy-start | bytes 100
